TPU v7x, 32 devices: a whole 2x2x4 slice. The times are simulated.
32 devices in a mesh: dp: 8 (over y, x, core), seq: 4 (over z).
Axes of the slice: x: 2, y: 2, z: 4, core: 2. Of those that a mesh axis runs over, the one named last changes fastest.
Arguments:
- tokens: bfloat16 [16, 2048, 768], P('dp', 'seq'), may hold values from -6 to 6
- segment_ids: int32 [16, 2048], P('dp', 'seq'), may hold values from 0 to 3, never falling along the last dimension, each value on 1 to 1024 neighbouring positions
- boundary_mask: int32 [16, 4, 256], P('dp'), may hold values from 0 to 1, as said below
- w_qkv: bfloat16 [768, 2304], replicated, may hold values from -0.21875 to 0.21875
- b_qkv: float32 [2304], replicated, may hold values from -3 to 3
- w_out: bfloat16 [768, 768], replicated, may hold values from -1.75 to 1.75
- b_out: float32 [768], replicated, may hold values from -3 to 3
- ln1_gain: float32 [768], replicated, may hold values from 0.1 to 1.9
- ln1_bias: float32 [768], replicated, may hold values from -3 to 3
- w_in: bfloat16 [768, 3072], replicated, may hold values from -0.21875 to 0.21875
- b_in: float32 [3072], replicated, may hold values from -3 to 3
- w_down: bfloat16 [3072, 768], replicated, may hold values from -0.109375 to 0.109375
- b_down: float32 [768], replicated, may hold values from -3 to 3
- ln2_gain: float32 [768], replicated, may hold values from 0.1 to 1.9
- ln2_bias: float32 [768], replicated, may hold values from -3 to 3
- proj_e: bfloat16 [256, 2048], P(None, 'seq'), may hold values from -0.25 to 0.25
- cotangent: bfloat16 [16, 2048, 768], P('dp', 'seq'), may hold values from -6 to 6
Outputs:
- layer_out: bfloat16 [16, 2048, 768], P('dp', 'seq')
- grad_tokens: float32 [16, 2048, 768], P('dp', 'seq')
- grad_w_qkv: float32 [768, 2304], P(('dp', 'seq'))
- grad_b_qkv: float32 [2304], P(('dp', 'seq'))
- grad_w_out: float32 [768, 768], P(('dp', 'seq'))
- grad_b_out: float32 [768], P(('dp', 'seq'))
- grad_ln1_gain: float32 [768], P(('dp', 'seq'))
- grad_ln1_bias: float32 [768], P(('dp', 'seq'))
- grad_w_in: float32 [768, 3072], P(('dp', 'seq'))
- grad_b_in: float32 [3072], P(('dp', 'seq'))
- grad_w_down: float32 [3072, 768], P(('dp', 'seq'))
- grad_b_down: float32 [768], P(('dp', 'seq'))
- grad_ln2_gain: float32 [768], P(('dp', 'seq'))
- grad_ln2_bias: float32 [768], P(('dp', 'seq'))
- grad_proj_e: float32 [256, 2048], P(None, 'seq')
Inputs may be any that keep to these rules, and one draw needn't show every extreme that they name: `segment_ids`: each sequence's ids never fall; every one of the 4 segments has 1 to 1024 positions, and one has exactly 1024. `boundary_mask`: for each sequence, each of the 256 slots is owned by exactly one of its 4 segments, and each segment owns at least one slot.
All inputs are finite; a program needn't handle non-finite values.
Results may differ from a plain program's by a relative error of at most 0.02.
Values may be sent and summed in bfloat16 or wider, within the bound.
No kernel may reach another device: no remote copies, remote signals or barrier semaphores. Data moves between devices by JAX's collectives and lax.ppermute only.
A program may use at most 192 MiB of HBM per device.

v0:
```python
import functools

import jax
import jax.numpy as jnp
from jax import lax
from jax.experimental import pallas as pl
from jax.experimental.pallas import tpu as pltpu
from jax.sharding import PartitionSpec as P

HD = 64
KP = 256
NSEG = 4
TE = 272
EPS = 1e-05
SCALE = 0.125
HALF_ROOT = 0.7071067811865476
INV_ROOT_TAU = 0.3989422804014327
F32 = jnp.float32
BF16 = jnp.bfloat16
MIB = 2**20
VM = pl.BlockSpec(memory_space=pltpu.VMEM)
ANY = pl.BlockSpec(memory_space=pl.ANY)


def dot(left, right, cl=1, cr=0):
    return lax.dot_general(left, right, (((cl,), (cr,)), ((), ())), preferred_element_type=F32)


def in_vmem(x):
    return pltpu.with_memory_space_constraint(x, pltpu.VMEM)


def in_hbm(x):
    return pltpu.with_memory_space_constraint(x, pltpu.HBM)


def V(*shape, dtype=BF16):
    return pltpu.VMEM(shape, dtype)


def H(*shape, dtype=BF16):
    return pltpu.HBM(shape, dtype)


def call(kernel, name, args, outs, grid=(1,), in_specs=None, out_specs=None, scratch=(), limit=24, flops=0, nbytes=0, prefetch=()):
    placed = [{"v": in_vmem, "h": in_hbm, "n": lambda x: x}[where](x) for x, where, _ in args]
    default = {"v": VM, "h": ANY, "n": ANY}
    specs = [default[where] if spec is None else spec for _, where, spec in args]
    single = not isinstance(outs, list)
    if single:
        outs = [outs]
    shapes = [o for o, _ in outs]
    ospecs = [spec if spec is not None else VM for o, spec in outs]
    res = pl.pallas_call(
        kernel,
        tuple(shapes),
        grid_spec=pltpu.PrefetchScalarGridSpec(
            num_scalar_prefetch=len(prefetch),
            grid=grid,
            in_specs=specs,
            out_specs=tuple(ospecs),
            scratch_shapes=list(scratch),
        ),
        compiler_params=pltpu.CompilerParams(vmem_limit_bytes=limit * MIB),
        cost_estimate=pl.CostEstimate(flops=int(flops), bytes_accessed=int(nbytes), transcendentals=0),
        name=name,
    )(*prefetch, *placed)
    return res[0] if single else res


def block(shape, index):
    return pl.BlockSpec(shape, index)


def whole(shape):
    return pl.BlockSpec(shape, lambda *_: (0,) * len(shape))


def columns(row):
    return jnp.transpose(jnp.broadcast_to(row, (8, row.shape[-1])))[:, 0:1]


def prep_kernel(s, tok_ref, seg_ref, mask_ref, proj_ref, t_ref, al_ref, wt_ref):
    width = tok_ref.shape[-1]
    length = tok_ref.shape[1]
    m = mask_ref[0]
    owner = jnp.sum(m * lax.broadcasted_iota(jnp.int32, m.shape, 0), 0, keepdims=True).astype(F32)
    allowed = columns(owner) == seg_ref[s : s + 1, :].astype(F32)
    weighted = jnp.where(allowed, proj_ref[...].astype(F32), 0.0).astype(BF16)
    al_ref[...] = jnp.where(allowed, 1.0, 0.0).astype(BF16)
    wt_ref[...] = weighted
    t_ref[0:KP, :] = dot(weighted, tok_ref[0]).astype(BF16)
    count = dot(jnp.ones((TE - KP, length), BF16), weighted, 1, 1).astype(BF16)
    t_ref[KP:TE, :] = jnp.concatenate([count, jnp.zeros((TE - KP, width - KP), BF16)], 1)


def prep(s, tokens, segment_ids, mask, proj_e):
    seqs, length, width = tokens.shape
    return call(
        functools.partial(prep_kernel, s),
        "prep",
        [
            (tokens, "h", block((1, length, width), lambda i: (s, 0, 0))),
            (segment_ids, "h", whole((seqs, length))),
            (mask, "h", block((1, NSEG, KP), lambda i: (s, 0, 0))),
            (proj_e, "h", whole((KP, length))),
        ],
        [(H(TE, width), whole((TE, width))), (H(KP, length), whole((KP, length))), (H(KP, length), whole((KP, length)))],
        limit=5,
        flops=2 * KP * length * width,
        nbytes=2 * length * width,
    )


def query_kernel(me_ref, tok_ref, wq_ref, bq_ref, win_hbm, wdn_hbm, wo_hbm, q_ref, tt_ref, win_ref, wdn_ref, wo_ref, sem):
    pairs = ((wo_hbm, wo_ref), (win_hbm, win_ref), (wdn_hbm, wdn_ref))
    loads = [pltpu.make_async_copy(a, b, sem.at[k]) for k, (a, b) in enumerate(pairs)]

    @pl.when(pl.program_id(0) == 0)
    def _():
        for c in loads:
            c.start()

    units, rows = 2 * tt_ref.shape[1], tt_ref.shape[3]
    tok = tok_ref[0]
    q = (dot(tok, wq_ref[...]) + bq_ref[...]).astype(BF16).astype(F32) * SCALE
    q_ref[0] = jnp.transpose(q.astype(BF16))
    tt = jnp.transpose(tok)
    for u in range(units):
        r = u ^ me_ref[0]
        tt_ref[0, r >> 1, r & 1] = tt[u * rows : (u + 1) * rows]

    @pl.when(pl.program_id(0) == pl.num_programs(0) - 1)
    def _():
        for c in loads:
            c.wait()


def query(me, units, tokens, w_qkv, b_qkv, w_in, w_down, w_out):
    seqs, length, width = tokens.shape
    rows = width // units
    return call(
        query_kernel,
        "query",
        [
            (tokens, "h", block((1, length, width), lambda s, me: (s, 0, 0))),
            (w_qkv, "h", block((width, width), lambda s, me: (0, 0))),
            (b_qkv, "h", block((1, width), lambda s, me: (0, 0))),
            (w_in, "h", None),
            (w_down, "h", None),
            (w_out, "h", None),
        ],
        [
            (H(seqs, width, length), block((1, width, length), lambda s, me: (s, 0, 0))),
            (H(seqs, units // 2, 2, rows, length), block((1, units // 2, 2, rows, length), lambda s, me: (s, 0, 0, 0, 0))),
            (V(*w_in.shape), None),
            (V(*w_down.shape), None),
            (V(*w_out.shape), None),
        ],
        grid=(seqs,),
        prefetch=(me,),
        scratch=[pltpu.SemaphoreType.DMA((3,))],
        limit=10,
        flops=2 * seqs * width * length * width,
        nbytes=6 * seqs * length * width,
    )


def flip_kernel(w_ref, b_ref, bin_ref, o_ref, c_ref, cin_ref):
    o_ref[pl.program_id(0)] = jnp.transpose(w_ref[...])

    @pl.when(pl.program_id(0) == 0)
    def _():
        width = w_ref.shape[0]
        c_ref[...] = columns(b_ref[:, width:])
        cin_ref[...] = columns(bin_ref[...])


def flip(w_qkv, b_qkv, b_in):
    width = w_qkv.shape[0]
    ff = b_in.shape[1]
    return call(
        flip_kernel,
        "flip",
        [
            (w_qkv, "h", block((width, width), lambda i: (0, 1 + i))),
            (b_qkv, "h", whole((1, 3 * width))),
            (b_in, "h", whole((1, ff))),
        ],
        [(V(2, width, width), None), (V(2 * width, 1, dtype=F32), None), (V(ff, 1, dtype=F32), None)],
        grid=(2,),
        limit=6,
        nbytes=8 * width * width,
    )


def norm_stats(resid):
    center = resid - jnp.mean(resid, -1, keepdims=True)
    inverse = lax.rsqrt(jnp.mean(center * center, -1, keepdims=True) + EPS)
    return center * inverse, inverse


ROWS = 32
LANES = 128
GROUP = 4
LN_ROWS = 128
SMALL = (1, 1, 1, 1, 1, 1, 1, 1, 3, 4)


def attend_kernel(nt, s, me_ref, *refs):
    t_hbm = refs[:nt]
    wkv_ref, bkv_ref, q_hbm, al_ref, tok_ref, wo_ref, vec_ref = refs[nt : nt + 7]
    tt_ref, c_ref, kv_ref, p_hbm, att_ref, n_ref, inv_ref = refs[nt + 7 : nt + 14]
    t_scr, q_scr, p_scr, res_scr, att_scr, bias_scr, in_sem, out_sem = refs[nt + 14 :]
    width = wo_ref.shape[0]
    length = q_scr.shape[1]
    heads = width // HD
    units, rows = 2 * tt_ref.shape[0], tt_ref.shape[2]
    loads = [pltpu.make_async_copy(t_hbm[k], t_scr.at[k], in_sem.at[k]) for k in range(nt)]
    loads.append(pltpu.make_async_copy(q_hbm.at[s], q_scr, in_sem.at[nt]))
    for c in loads:
        c.start()
    bias_scr[...] = (al_ref[...].astype(F32) - 1.0) * 1e30
    for c in loads[:nt]:
        c.wait()
    total = t_scr[0].astype(F32)
    for k in range(1, nt):
        total = total + t_scr[k].astype(F32)
    low = total.astype(BF16)
    t_low = low[0:KP]
    c_row = low[KP : KP + 8, 0:KP]
    c_ref[...] = c_row
    wide_c = c_row[0:1].astype(F32)
    for k in range(2):
        part = slice(k * width, (k + 1) * width)
        kv_ref[part, :] = (dot(wkv_ref[k], t_low, 1, 1) + bkv_ref[part, :] * wide_c).astype(BF16)
    tt = jnp.transpose(t_low)
    me = me_ref[0]
    for u in range(units):
        r = u ^ me
        tt_ref[r >> 1, r & 1] = tt[u * rows : (u + 1) * rows]
    loads[nt].wait()

    def store(g):
        part = pl.ds(g * GROUP, GROUP)
        return pltpu.make_async_copy(p_scr.at[part], p_hbm.at[part], out_sem.at[g])

    tiles = [(h, j) for h in range(GROUP) for j in range(length // LANES)]

    def heads_of(g, carry):
        keys = {}

        def cut(h, shift=0):
            return pl.ds(pl.multiple_of(shift + (g * GROUP + h) * HD, HD), HD)

        def score(h, j):
            if j == 0:
                keys[h] = jnp.transpose(kv_ref[cut(h), :])
            return dot(keys[h], q_scr[cut(h), j * LANES : (j + 1) * LANES])

        scores = score(*tiles[0])
        for i, (h, j) in enumerate(tiles):
            after = score(*tiles[i + 1]) if i + 1 < len(tiles) else None
            where = slice(j * LANES, (j + 1) * LANES)
            scores = scores + bias_scr[:, where]
            expo = jnp.exp(scores - jnp.max(scores, 0, keepdims=True))
            p_scr[g * GROUP + h, :, where] = (expo * (1.0 / jnp.sum(expo, 0, keepdims=True))).astype(BF16)
            if j == length // LANES - 1:
                att_scr[cut(h), :] = dot(kv_ref[cut(h, width), :], p_scr[g * GROUP + h]).astype(BF16)
            scores = after
        store(g).start()
        return carry

    lax.fori_loop(0, heads // GROUP, heads_of, 0)
    att = att_scr[...]
    res_scr[...] = dot(att, wo_ref[...], 0, 0)
    for u in range(units):
        r = u ^ me
        att_ref[r >> 1, r & 1] = att_scr[u * rows : (u + 1) * rows, :]

    def tile(i, carry):
        part = pl.ds(pl.multiple_of(i * LN_ROWS, LN_ROWS), LN_ROWS)
        normed, inverse = norm_stats(res_scr[part, :] + tok_ref[0, part, :].astype(F32) + vec_ref[0:1, :])
        n_ref[part, :] = normed
        inv_ref[part, :] = inverse
        return carry

    lax.fori_loop(0, length // LN_ROWS, tile, 0)
    for g in range(heads // GROUP):
        store(g).wait()


def attend(me, s, units, others, wkv_t, bkv_col, q_t, allow, tokens, w_out, vecs):
    seqs, length, width = tokens.shape
    rows = width // units
    heads = width // HD
    nt = len(others)
    return call(
        functools.partial(attend_kernel, nt, s),
        "attend",
        [(t, "n", None) for t in others]
        + [
            (wkv_t, "v", None),
            (bkv_col, "v", None),
            (q_t, "h", None),
            (allow, "h", whole((KP, length))),
            (tokens, "h", block((1, length, width), lambda i, me: (s, 0, 0))),
            (w_out, "v", None),
            (vecs, "h", whole(vecs.shape)),
        ],
        [
            (V(units // 2, 2, rows, KP), None),
            (V(8, KP), None),
            (V(2 * width, KP), None),
            (H(heads, KP, length), ANY),
            (V(units // 2, 2, rows, length), None),
            (V(length, width, dtype=F32), None),
            (V(length, 1, dtype=F32), None),
        ],
        prefetch=(me,),
        scratch=[
            pltpu.VMEM((nt, TE, width), BF16),
            pltpu.VMEM((width, length), BF16),
            pltpu.VMEM((heads, KP, length), BF16),
            pltpu.VMEM((length, width), F32),
            pltpu.VMEM((width, length), BF16),
            pltpu.VMEM((KP, length), F32),
            pltpu.SemaphoreType.DMA((nt + 1,)),
            pltpu.SemaphoreType.DMA((heads,)),
        ],
        limit=12,
        flops=2 * KP * width * 2 * width + 8 * KP * length * width + 2 * length * width * width,
        nbytes=10 * MIB,
    )


def norm_back(upstream, normed, inverse, gain):
    scaled = upstream * gain
    return inverse * (
        scaled
        - jnp.mean(scaled, -1, keepdims=True)
        - normed * jnp.mean(scaled * normed, -1, keepdims=True)
    )


FR = 16


def feed_kernel(
    steps, me_ref, n_ref, inv_ref, vec_ref, win_ref, bin_ref, wdn_ref, cot_ref,
    mt_ref, at_ref, gb_ref, dh_ref, out_ref, gf_ref, gfl_ref, stat_ref,
    low_scr, acc_scr, slope_scr, h0_scr, h1_scr,
):
    step = pl.program_id(0)
    g1_ref, be1_ref, bdn_ref, g2_ref, be2_ref = [vec_ref.at[k : k + 1, :] for k in range(1, 6)]
    me = me_ref[0]
    units, rows = 2 * mt_ref.shape[0], mt_ref.shape[2]
    arows = at_ref.shape[2]
    length, width = n_ref.shape
    half = h0_scr.shape[0]
    per = half // arows

    @pl.when(step == 0)
    def _():
        for r in range(0, length, ROWS):
            part = slice(r, r + ROWS)
            mid = n_ref[part, :] * g1_ref[...] + be1_ref[...]
            low_scr[part, :] = mid.astype(BF16)
            acc_scr[part, :] = mid + bdn_ref[...]
        mt = jnp.transpose(low_scr[...])
        for u in range(units):
            r = u ^ me
            mt_ref[r >> 1, r & 1] = mt[u * rows : (u + 1) * rows]

    def unit(base, i):
        r = (base + i) ^ me
        return r >> 1, r & 1

    @pl.when(step < steps)
    def _():
        base = step * 2 * per

        def gelu(k, h_scr):
            for f in range(0, half, FR):
                at = k * half + f
                hidden = h_scr[f : f + FR, :] + bin_ref[pl.ds(pl.multiple_of(step * 2 * half + at, FR), FR), :]
                phi = 0.5 + 0.5 * lax.erf(hidden * HALF_ROOT)
                bell = jnp.exp(-0.5 * hidden * hidden)
                hi, lo = unit(base, at // arows)
                at_ref[hi, lo, at % arows : at % arows + FR, :] = (hidden * phi).astype(BF16)
                slope_scr[step, at : at + FR, :] = (phi + (hidden * INV_ROOT_TAU) * bell).astype(BF16)

        def cut(k):
            return pl.ds(pl.multiple_of(step * 2 * half + k * half, half), half)

        def second(k):
            activ = jnp.concatenate([at_ref[unit(base, k * per + i)] for i in range(per)], 0)
            acc_scr[...] += dot(activ, wdn_ref[cut(k), :], 0, 0)

        low = low_scr[...]
        h0_scr[...] = dot(win_ref[:, cut(0)], low, 0, 1)
        h1_scr[...] = dot(win_ref[:, cut(1)], low, 0, 1)
        gelu(0, h0_scr)
        second(0)
        gelu(1, h1_scr)
        second(1)

    @pl.when(step == steps - 1)
    def _():
        def tile(i, sums):
            part = pl.ds(pl.multiple_of(i * LN_ROWS, LN_ROWS), LN_ROWS)
            normed, inverse = norm_stats(acc_scr[part, :])
            out_ref[part, :] = (normed * g2_ref[...] + be2_ref[...]).astype(BF16)
            cot = cot_ref[0, part, :].astype(F32)
            second = norm_back(cot, normed, inverse, g2_ref[...])
            low = second.astype(BF16)
            gb_ref[part, :] = low
            acc_scr[part, :] = second
            terms = (cot * normed, cot, low.astype(F32))
            return tuple(a + jnp.sum(t, 0, keepdims=True) for a, t in zip(sums, terms))

        sums = lax.fori_loop(0, length // LN_ROWS, tile, (jnp.zeros((1, width), F32),) * 3)
        for k in range(3):
            stat_ref[k : k + 1, :] = sums[k]

    @pl.when(step >= steps)
    def _():
        back = step - steps
        gb = gb_ref[...]

        def slope(k, h_scr):
            for f in range(0, half, FR):
                at = k * half + f
                dh = (h_scr[f : f + FR, :] * slope_scr[back, at : at + FR, :].astype(F32)).astype(BF16)
                row = pl.ds(pl.multiple_of(back * 2 * half + at, FR), FR)
                dh_ref[row, :] = dh

        def cut(k):
            return pl.ds(pl.multiple_of(back * 2 * half + k * half, half), half)

        def down(k):
            acc_scr[...] += dot(dh_ref[cut(k), :], win_ref[:, cut(k)], 0, 1)

        h0_scr[...] = dot(wdn_ref[cut(0), :], gb, 1, 1)
        h1_scr[...] = dot(wdn_ref[cut(1), :], gb, 1, 1)
        slope(0, h0_scr)
        down(0)
        slope(1, h1_scr)
        down(1)

    @pl.when(step == 2 * steps - 1)
    def _():
        def tile(i, sums):
            part = pl.ds(pl.multiple_of(i * LN_ROWS, LN_ROWS), LN_ROWS)
            up = acc_scr[part, :]
            normed = n_ref[part, :]
            first = norm_back(up, normed, inv_ref[part, :], g1_ref[...])
            low = first.astype(BF16)
            gf_ref[part, :] = first
            gfl_ref[part, :] = low
            terms = (up * normed, up, low.astype(F32))
            return tuple(a + jnp.sum(t, 0, keepdims=True) for a, t in zip(sums, terms))

        sums = lax.fori_loop(0, length // LN_ROWS, tile, (jnp.zeros((1, width), F32),) * 3)
        for k in range(3):
            stat_ref[3 + k : 4 + k, :] = sums[k]
        stat_ref[6:8, :] = jnp.zeros((2, width), F32)


def feed(me, s, units, normed, inverse, vecs, w_in, bin_col, w_down, cot):
    length, width = normed.shape
    ff = w_in.shape[1]
    rows = width // units
    arows = ff // units
    chunk = 768
    steps = ff // chunk
    return call(
        functools.partial(feed_kernel, steps),
        "feed",
        [
            (normed, "v", None),
            (inverse, "v", None),
            (vecs, "h", whole(vecs.shape)),
            (w_in, "v", None),
            (bin_col, "v", None),
            (w_down, "v", None),
            (cot, "h", block((1, length, width), lambda i, me: (s, 0, 0))),
        ],
        [
            (V(units // 2, 2, rows, length), None),
            (V(units // 2, 2, arows, length), None),
            (V(length, width), None),
            (V(ff, length), None),
            (H(length, width), whole((length, width))),
            (H(length, width, dtype=F32), whole((length, width))),
            (H(length, width), whole((length, width))),
            (V(8, width, dtype=F32), None),
        ],
        grid=(2 * steps,),
        prefetch=(me,),
        scratch=[
            pltpu.VMEM((length, width), BF16),
            pltpu.VMEM((length, width), F32),
            pltpu.VMEM((steps, chunk, length), BF16),
            pltpu.VMEM((chunk // 2, length), F32),
            pltpu.VMEM((chunk // 2, length), F32),
        ],
        limit=18,
        flops=8 * length * width * ff,
        nbytes=24 * MIB,
    )


def attend_back_kernel(seqs, *refs):
    gfl_hbm, kv_hbm, p_hbm, c_refs = [refs[k * seqs : (k + 1) * seqs] for k in range(4)]
    wo_ref, q_hbm, wkv_ref, bkv_ref, dq_ref, gs_ref, gt_ref, col_ref = refs[4 * seqs : 4 * seqs + 8]
    gfl_scr, kv_scr, p_scr, q_scr, c_scr, da_scr, ds0_scr, ds1_scr, sem, p_sem = refs[4 * seqs + 8 :]
    s = pl.program_id(0)
    width = wo_ref.shape[0]
    length = gfl_scr.shape[1]
    heads = width // HD
    groups = heads // GROUP

    def inputs(k):
        pairs = ((gfl_hbm[k], gfl_scr.at[k]), (q_hbm.at[k], q_scr.at[k]), (kv_hbm[k], kv_scr.at[k]))
        return [pltpu.make_async_copy(x, y, sem.at[k, i]) for i, (x, y) in enumerate(pairs)]

    def load(k, g):
        part = pl.ds(g * GROUP, GROUP)
        return pltpu.make_async_copy(p_hbm[k].at[part], p_scr.at[k, part], p_sem.at[k, g])

    @pl.when(s == 0)
    def _():
        for k in range(seqs):
            for c in inputs(k):
                c.start()
            for g in range(groups):
                load(k, g).start()

    for k in range(seqs):

        @pl.when(s == k)
        def _(k=k):
            c_scr[...] = c_refs[k][...]
            for c in inputs(k):
                c.wait()
            for g in range(groups):
                load(k, g).wait()

    da_scr[...] = dot(wo_ref[...], gfl_scr[s], 1, 1).astype(BF16)
    c_wide = c_scr[0:1, :].astype(F32)
    tiles = [(h, j) for h in range(GROUP) for j in range(length // LANES)]

    def heads_of(g, carry):
        vals = {}

        def cut(h, shift=0):
            return pl.ds(pl.multiple_of(shift + (g * GROUP + h) * HD, HD), HD)

        def first(h, j):
            if j == 0:
                vals[h] = jnp.transpose(kv_scr[s, cut(h, width), :])
            return dot(vals[h], da_scr[cut(h), j * LANES : (j + 1) * LANES])

        grad = first(*tiles[0])
        for i, (h, j) in enumerate(tiles):
            after = first(*tiles[i + 1]) if i + 1 < len(tiles) else None
            where = slice(j * LANES, (j + 1) * LANES)
            ds_scr = (ds0_scr, ds1_scr)[h % 2]
            wide = p_scr[s, g * GROUP + h, :, where].astype(F32)
            prod = wide * grad
            ds_scr[:, where] = (prod - wide * jnp.sum(prod, 0, keepdims=True)).astype(BF16)
            if j == length // LANES - 1:
                gv = dot(da_scr[cut(h), :], p_scr[s, g * GROUP + h], 1, 1).astype(BF16)
                gs_ref[s, cut(h, width), :] = gv
                col_ref[s, cut(h, 2 * width), :] = jnp.sum(gv.astype(F32) * c_wide, 1, keepdims=True)
                dq = (dot(kv_scr[s, cut(h), :], ds_scr[...]) * SCALE).astype(BF16)
                dq_ref[s, cut(h), :] = dq
                col_ref[s, cut(h), :] = jnp.sum(dq.astype(F32), 1, keepdims=True)
                gk = dot(q_scr[s, cut(h), :], ds_scr[...], 1, 1).astype(BF16)
                gs_ref[s, cut(h), :] = gk
                col_ref[s, cut(h, width), :] = jnp.sum(gk.astype(F32) * c_wide, 1, keepdims=True)
            grad = after
        return carry

    lax.fori_loop(0, groups, heads_of, 0)
    gs = gs_ref[s]
    gt = dot(gs[0:width], wkv_ref[0], 0, 0) + dot(gs[width:], wkv_ref[1], 0, 0)
    gt_ref[0, 0:KP, :] = gt.astype(BF16)
    pad = TE - KP
    b_hi = bkv_ref[...].astype(BF16)
    b_lo = (bkv_ref[...] - b_hi.astype(F32)).astype(BF16)
    drow = dot(jnp.broadcast_to(b_hi, (pad, 2 * width)), gs) + dot(jnp.broadcast_to(b_lo, (pad, 2 * width)), gs)
    gt_ref[0, KP:TE, :] = jnp.concatenate([drow.astype(BF16), jnp.zeros((pad, width - KP), BF16)], 1)


def attend_back(gfl, w_out, kv_t, probs, q_t, c_row, wkv_t, bkv_row):
    seqs = len(gfl)
    length, width = gfl[0].shape
    heads = width // HD
    return call(
        functools.partial(attend_back_kernel, seqs),
        "attend_back",
        [(x, "n", None) for x in (*gfl, *kv_t, *probs)]
        + [(c, "v", None) for c in c_row]
        + [
            (w_out, "v", None),
            (q_t, "h", None),
            (wkv_t, "v", None),
            (bkv_row, "h", whole((1, 2 * width))),
        ],
        [
            (V(seqs, width, length), None),
            (V(seqs, 2 * width, KP), None),
            (H(seqs, TE, width), block((1, TE, width), lambda s: (s, 0, 0))),
            (V(seqs, 3 * width, 1, dtype=F32), None),
        ],
        grid=(seqs,),
        scratch=[
            pltpu.VMEM((seqs, length, width), BF16),
            pltpu.VMEM((seqs, 2 * width, KP), BF16),
            pltpu.VMEM((seqs, heads, KP, length), BF16),
            pltpu.VMEM((seqs, width, length), BF16),
            pltpu.VMEM((8, KP), BF16),
            pltpu.VMEM((width, length), BF16),
            pltpu.VMEM((KP, length), BF16),
            pltpu.VMEM((KP, length), BF16),
            pltpu.SemaphoreType.DMA((seqs, 3)),
            pltpu.SemaphoreType.DMA((seqs, heads // GROUP)),
        ],
        limit=22,
        flops=(2 * KP * width * 2 * width + 16 * KP * length * width + 2 * length * width * width) // 1024,
        nbytes=1024,
    )


def token_kernel(gf_refs, dq_ref, wq_ref, o_ref):
    for k, g in enumerate(gf_refs):
        o_ref[k] = g[...] + dot(dq_ref[k], wq_ref[...], 0, 1)


def token_grad(gf, dq_t, w_qkv):
    seqs = len(gf)
    length, width = gf[0].shape
    shape = (seqs, length, width)
    return call(
        lambda *refs: token_kernel(refs[:seqs], *refs[seqs:]),
        "token_grad",
        [(g, "h", whole((length, width))) for g in gf]
        + [(dq_t, "v", None), (w_qkv, "h", block((width, width), lambda i: (0, 0)))],
        (H(*shape, dtype=F32), whole(shape)),
        limit=16,
        flops=seqs * length * width * width // 1024,
        nbytes=1024,
    )


def last_kernel(nt, *refs):
    t_refs = refs[:nt]
    part_ref, wt_ref, al_ref, tok_ref, o_ref, gp_ref, d_scr = refs[nt:]
    s = pl.program_id(0)
    total = t_refs[0][0].astype(F32)
    for r in t_refs[1:]:
        total = total + r[0].astype(F32)
    low = total[0:KP].astype(BF16)
    d_col = columns(total[KP : KP + 1, 0:KP])
    o_ref[0] = part_ref[0] + dot(wt_ref[0], low, 0, 0)
    term = (dot(low, tok_ref[0], 1, 1) + d_col) * al_ref[0].astype(F32)

    @pl.when(s == 0)
    def _():
        d_scr[...] = term

    @pl.when(s > 0)
    def _():
        d_scr[...] = d_scr[...] + term

    @pl.when(s == pl.num_programs(0) - 1)
    def _():
        gp_ref[...] = d_scr[...].astype(BF16)


def last(tparts, parts, weights, allows, tokens):
    seqs, length, width = tokens.shape
    each = lambda *shape: block((1, *shape), lambda s: (s,) + (0,) * len(shape))
    return call(
        functools.partial(last_kernel, len(tparts)),
        "last",
        [(t, "n", each(TE, width)) for t in tparts]
        + [(parts, "h", each(length, width)), (weights, "h", each(KP, length)), (allows, "h", each(KP, length)), (tokens, "h", each(length, width))],
        [(H(seqs, length, width, dtype=F32), each(length, width)), (H(KP, length), whole((KP, length)))],
        grid=(seqs,),
        scratch=[pltpu.VMEM((KP, length), F32)],
        limit=18,
        flops=4 * seqs * length * width * KP,
        nbytes=8 * MIB,
    )


def split_store(low, send_ref, keep_ref, send_bit, where):
    n = low.shape[0]
    if send_bit == 0:
        for i in range(n):
            (send_ref if i & 1 else keep_ref)[i // 2, :, where] = low[i]
    else:
        half = n // 2
        keep_ref[:, :, where] = low[:half]
        send_ref[:, :, where] = low[half:]


def total(terms):
    out = terms[0]
    for t in terms[1:]:
        out = out + t
    return out


def down_kernel(seqs, core, chunk, send_bit, *refs):
    at_refs = refs[:seqs]
    gb_refs = refs[seqs : 2 * seqs]
    rest = refs[2 * seqs :]
    n, _, arows, length = at_refs[0].shape
    cols = pl.ds(pl.multiple_of(pl.program_id(0) * chunk, chunk), chunk)
    res = total([dot(a[:, core].reshape(n * arows, length), g[:, cols]) for a, g in zip(at_refs, gb_refs)])
    res = res.reshape(n, arows, chunk)
    if send_bit is None:
        rest[0][...] = res.astype(BF16)
    else:
        recv_ref, send_ref, keep_ref = rest
        low = (res + recv_ref[...].astype(F32)).astype(BF16)
        split_store(low, send_ref, keep_ref, send_bit, slice(None))


def down_grad(at, gb, core, recv=None, send_bit=None):
    seqs = len(at)
    n, _, arows, length = at[0].shape
    width = gb[0].shape[1]
    chunk = 256
    args = [(a, "v", None) for a in at] + [(g, "v", None) for g in gb]
    spec = block((n, arows, chunk), lambda i: (0, 0, i))
    if recv is None:
        outs = (H(n, arows, width), spec)
    else:
        args.append((recv, "n", spec))
        outs = [(H(n // 2, arows, width), block((n // 2, arows, chunk), lambda i: (0, 0, i)))] * 2
    return call(
        functools.partial(down_kernel, seqs, core, chunk, send_bit),
        "down_grad",
        args,
        outs,
        grid=(width // chunk,),
        limit=12,
        flops=2 * seqs * n * arows * length * width,
        nbytes=3 * MIB,
    )


def in_kernel(seqs, core, chunk, send_bit, *refs):
    mt_refs = refs[:seqs]
    dh_refs = refs[seqs : 2 * seqs]
    rest = refs[2 * seqs :]
    n, _, rows, length = mt_refs[0].shape
    part = pl.ds(pl.multiple_of(pl.program_id(0) * chunk, chunk), chunk)
    lefts = [a[:, core].reshape(n * rows, length) for a in mt_refs]
    if send_bit is None:
        lefts = [jnp.concatenate([a, jnp.ones((16, length), BF16)], 0) for a in lefts]
    res = total([dot(a, g[part, :], 1, 1) for a, g in zip(lefts, dh_refs)])
    if send_bit is None:
        out_ref, bias_ref = rest
        out_ref[...] = res[0 : n * rows].reshape(n, rows, chunk).astype(BF16)
        bias_ref[...] = res[n * rows : n * rows + 8]
    else:
        res = res.reshape(n, rows, chunk)
        recv_ref, send_ref, keep_ref = rest
        low = (res + recv_ref[...].astype(F32)).astype(BF16)
        split_store(low, send_ref, keep_ref, send_bit, slice(None))


def in_grad(mt, dh, core, recv=None, send_bit=None):
    seqs = len(mt)
    n, _, rows, length = mt[0].shape
    ff = dh[0].shape[0]
    chunk = 1536
    args = [(a, "v", None) for a in mt] + [(g, "v", None) for g in dh]
    spec = block((n, rows, chunk), lambda i: (0, 0, i))
    if recv is None:
        outs = [(H(n, rows, ff), spec), (H(8, ff, dtype=F32), block((8, chunk), lambda i: (0, i)))]
    else:
        args.append((recv, "n", spec))
        outs = [(H(n // 2, rows, ff), block((n // 2, rows, chunk), lambda i: (0, 0, i)))] * 2
    return call(
        functools.partial(in_kernel, seqs, core, chunk, send_bit),
        "in_grad",
        args,
        outs,
        grid=(ff // chunk,),
        limit=12,
        flops=2 * seqs * n * rows * length * ff,
        nbytes=3 * MIB,
    )


def pack_stats(stat_refs, bias_refs, col_refs, scr, bias_scr, group):
    rows = scr.shape[0]
    scr[...] = jnp.zeros_like(scr)
    stat = total([r[...] for r in stat_refs])
    scr[:, 0:8] = jnp.transpose(stat)
    bias_scr[...] = jnp.transpose(total([r[...] for r in bias_refs]))[:, 0:1]
    lane = 8
    for refs in (col_refs, [bias_scr]):
        per = refs[0].shape[0] // rows
        for b in range(rows // group):
            for c in range(per):
                src = slice((b * per + c) * group, (b * per + c + 1) * group)
                scr[b * group : (b + 1) * group, lane + c : lane + c + 1] = total([r[src, :] for r in refs])
        lane += per


def rest_kernel(seqs, group, me_ref, *refs):
    at_refs, gf_refs, tk_refs, tt_refs = [refs[k * seqs : (k + 1) * seqs] for k in range(4)]
    dq_refs, gs_refs = [[refs[4 * seqs + k].at[i] for i in range(seqs)] for k in range(2)]
    rest = refs[4 * seqs + 2 :]
    keep_ref, send_ref, st_scr, bias_scr = rest[-4:]
    n, _, rows, _ = at_refs[0].shape
    width = gf_refs[0].shape[1]

    def put(res, where):
        res = res.reshape(n, 2, rows, res.shape[-1]).astype(BF16)
        keep_ref[:, :, where] = res[:, 0]
        send_ref[:, :, where] = res[:, 1]

    def flat(ref):
        return ref[...].reshape(2 * n * rows, ref.shape[-1])

    if group:
        pack_stats(rest[:seqs], [rest[seqs]], [rest[seqs + 1].at[k] for k in range(seqs)], st_scr, bias_scr, group)
        for u in range(2 * n):
            low = st_scr[pl.ds(pl.multiple_of((u ^ me_ref[0]) * rows, rows), rows), :].astype(BF16)
            (keep_ref, send_ref)[u % 2][u // 2, :, 4 * width : 4 * width + 128] = low
    else:
        for ref in (keep_ref, send_ref):
            ref[:, :, 4 * width : 4 * width + 128] = jnp.zeros((n, rows, 128), BF16)
    put(total([dot(flat(a), g[...]) for a, g in zip(at_refs, gf_refs)]), slice(0, width))
    put(total([dot(flat(a), g[...], 1, 1) for a, g in zip(tk_refs, dq_refs)]), slice(width, 2 * width))
    for k in range(2):
        part = slice(k * width, (k + 1) * width)
        put(total([dot(flat(a), g[part, :], 1, 1) for a, g in zip(tt_refs, gs_refs)]), slice((2 + k) * width, (3 + k) * width))


def rest_grad(me, att, gfl, tok_t, dq_t, t_t, gs_t, group, stats):
    seqs = len(att)
    n, _, rows, length = att[0].shape
    width = gfl[0].shape[1]
    cols = 4 * width + 128
    args = [(a, "v", None) for a in att] + [(g, "h", whole((length, width))) for g in gfl]
    args += [(t, "h", block((pl.Squeezed(), n, 2, rows, length), lambda i, me, k=k: (k, 0, 0, 0, 0))) for k, t in enumerate([tok_t] * seqs)]
    args += [(a, "v", None) for a in (*t_t, dq_t, gs_t)]
    args += [(a, "v", None) for a in stats[0]] + [(stats[1], "h", whole(stats[1].shape)), (stats[2], "v", None)]
    return call(
        functools.partial(rest_kernel, seqs, group),
        "rest_grad",
        args,
        [(H(n, rows, cols), whole((n, rows, cols)))] * 2,
        prefetch=(me,),
        scratch=[pltpu.VMEM((2 * n * rows, 128), F32), pltpu.VMEM((stats[1].shape[1], 1), F32)],
        limit=16,
        flops=seqs * 2 * n * rows * (4 * length * width + 4 * KP * width) // 1024,
        nbytes=1024,
    )


def halve_kernel(z_ref, ka_ref, ra_ref, kb_ref, rb_ref, send_ref, keep_ref):
    z = z_ref[0]
    cut = ka_ref.shape[-1]
    for k in range(2):
        for keep, recv, cols in ((ka_ref, ra_ref, slice(0, cut)), (kb_ref, rb_ref, slice(cut, None))):
            for where, out in ((1 - z, send_ref), (z, keep_ref)):
                out[k, :, cols] = (keep[k, where].astype(F32) + recv[k, where].astype(F32)).astype(BF16)


def halve_rest(z, ka, ra, kb, rb):
    group = ka.shape[0] // 4
    arrays = [x.reshape(2, 2, group, x.shape[-1]) for x in (ka, ra, kb, rb)]
    cols = ka.shape[-1] + kb.shape[-1]
    shape = (2, group, cols)
    return call(
        halve_kernel,
        "halve_rest",
        [(x, "n", whole(x.shape)) for x in arrays],
        [(H(*shape), whole(shape)), (H(*shape), whole(shape))],
        prefetch=(z,),
        limit=6,
        nbytes=2 * MIB,
    )


def finish_kernel(z_ref, keep_ref, recv_ref, qkv_ref, out_ref, *small_refs):
    width = out_ref.shape[1]
    res = keep_ref[...].astype(F32) + recv_ref[...].astype(F32)
    out_ref[...] = res[:, 0:width]
    qkv_ref[...] = res[:, width : 4 * width]
    small = jnp.transpose(res[:, 4 * width :])
    lane = 0
    for ref, per in zip(small_refs, SMALL):
        parts = [small[lane + k : lane + k + 1, :] for k in range(per)]
        ref[...] = (jnp.concatenate(parts, 1) if per > 1 else parts[0]).reshape(ref.shape)
        lane += per


def finish_rest(z, keep, recv):
    group, cols = keep.shape
    width = (cols - 128) // 4
    return call(
        finish_kernel,
        "finish_rest",
        [(keep, "n", whole((group, cols))), (recv, "n", whole((group, cols)))],
        [
            (H(group, 3 * width, dtype=F32), whole((group, 3 * width))),
            (H(group, width, dtype=F32), whole((group, width))),
            *[(H(per * group, dtype=F32), whole((per * group,))) for per in SMALL],
        ],
        prefetch=(z,),
        limit=5,
        nbytes=MIB,
    )


def add(a, b):
    return (a.astype(F32) + b.astype(F32)).astype(BF16)


def body(n_dp, n_seq, tokens, segment_ids, mask, w_qkv, b_qkv, w_out, b_out, ln1_gain, ln1_bias, w_in, b_in, w_down, b_down, ln2_gain, ln2_bias, proj_e, cotangent):
    seqs, length, width = tokens.shape
    ff = w_in.shape[1]
    n_all = n_dp * n_seq
    fast = n_dp == 8 and n_seq == 4 and length >= 512
    units = 8
    dp = lax.axis_index("dp").astype(jnp.int32)
    sq = lax.axis_index("seq").astype(jnp.int32)
    me = (dp if fast else jnp.zeros((), jnp.int32)).reshape(1)
    row = lambda v: v.reshape(1, -1)

    def swap(x, bit):
        pairs = [(i, i ^ bit) for i in range(n_all)]
        return lax.ppermute(x, ("dp", "seq"), pairs)

    near = [(i, i ^ 1) for i in range(n_seq)]
    mid = [(1, 2), (2, 1)]

    def hop_one(own):
        return lax.ppermute(own, "seq", near), lax.ppermute(own, "seq", mid)

    def hop_two(first):
        return lax.ppermute(first[1], "seq", near), lax.ppermute(first[0], "seq", mid)

    def tie(x, *deps):
        return lax.optimization_barrier((x, *deps))[0]

    vecs = jnp.stack([b_out, ln1_gain, ln1_bias, b_down, ln2_gain, ln2_bias])
    first = prep(0, tokens, segment_ids, mask, proj_e)
    prepped = [first] + [prep(s, tie(tokens, first[0]), segment_ids, mask, proj_e) for s in range(1, seqs)]
    owns = [p[0] for p in prepped]
    wkv_t, bkv_col, bin_col = flip(tie(w_qkv, vecs, *owns), row(b_qkv), row(b_in))
    if fast:
        one = tuple(tie(x, wkv_t) for x in hop_one(owns[0]))
        q_t, tok_t, w_in, w_down, w_out = query(me, units, tie(tokens, wkv_t, *one), w_qkv, row(b_qkv), w_in, w_down, w_out)
        tparts = [[owns[0], *one, *(tie(x, q_t) for x in hop_two(one))]]
    else:
        q_t, tok_t, w_in, w_down, w_out = query(me, units, tie(tokens, wkv_t), w_qkv, row(b_qkv), w_in, w_down, w_out)
        tparts = [[lax.psum(o, "seq")] for o in owns]

    tt, crow, kv, probs, att, normed, inverse = [], [], [], [], [], [], []
    mt, at, gb, dh, outs, gf, gfl, stat = [], [], [], [], [], [], [], []
    for s in range(seqs):
        if s:
            tparts[s][0] = tie(tparts[s][0], gfl[s - 1])
        if fast and s + 1 < seqs:
            own = tie(owns[s + 1], q_t)
            one = hop_one(own)
        res = attend(me, s, units, tparts[s], wkv_t, bkv_col, q_t, prepped[s][1], tokens, w_out, vecs)
        for store, value in zip((tt, crow, kv, probs, att, normed, inverse), res):
            store.append(value)
        if fast and s + 1 < seqs:
            normed[s] = tie(normed[s], *one)
            tparts.append([own, *one, *hop_two(one)])
        res = feed(me, s, units, normed[s], inverse[s], vecs, w_in, bin_col, w_down, cotangent)
        for store, value in zip((mt, at, gb, dh, outs, gf, gfl, stat), res):
            store.append(value)

    X_BIT, Y_BIT, CORE = 2 * n_seq, 4 * n_seq, n_seq
    z0, z1 = sq & 1, sq >> 1

    def halve(recv, keep):
        return add(keep[1], recv[1]), add(keep[0], recv[0])

    def halve_z0(recv, keep):
        group = keep.shape[0] // 4
        shape = (2, 2, group, keep.shape[-1])
        pick = lambda a, z: lax.dynamic_index_in_dim(a, z, 1, keepdims=False)
        keep, recv = keep.reshape(shape), recv.reshape(shape)
        return add(pick(keep, 1 - z0), pick(recv, 1 - z0)), add(pick(keep, z0), pick(recv, z0))

    def halve_z1(recv, keep):
        pick = lambda a, z: lax.dynamic_index_in_dim(a, z, 0, keepdims=False)
        return add(pick(keep, 1 - z1), pick(recv, 1 - z1)), add(pick(keep, z1), pick(recv, z1))

    back_in = list(gfl)
    if fast:
        send1 = down_grad(at, gb, 1)
        recv1 = swap(send1, CORE)
        send2, gbin = in_grad([tie(mt[0], send1), *mt[1:]], dh, 1)
        recv2 = swap(send2, CORE)
        sx1, kx1 = down_grad([tie(at[0], send2), *at[1:]], gb, 0, recv1, 0)
        rx1 = swap(sx1, X_BIT)
        sx2, kx2 = in_grad([tie(mt[0], sx1), *mt[1:]], dh, 0, recv2, 1)
        rx2 = swap(sx2, Y_BIT)
        back_in[0] = tie(gfl[0], sx2)

    dq_t, gs_t, gsum, col = attend_back(back_in, w_out, kv, probs, q_t, crow, wkv_t, row(b_qkv[width:]))
    if not fast:
        half2, gbin = in_grad(mt, dh, 1)
    stats = (stat, gbin, col)

    if fast:
        group = width // n_all
        gone = hop_one(gsum)
        parts = token_grad(gf, dq_t, w_qkv)
        sy1, ky1 = halve(tie(rx1, parts), kx1)
        ry1 = swap(sy1, Y_BIT)
        sy2, ky2 = halve(tie(rx2, parts), kx2)
        ry2 = swap(sy2, X_BIT)
        keep3, send3 = rest_grad(me, [tie(att[0], sy1, sy2, parts, gsum), *att[1:]], gfl, tok_t, dq_t, tt, gs_t, group, stats)
        recv3 = swap(tie(send3, ry1, ry2, *gone), CORE)
        half, cut = units // 4, 2 * width
        pair = lambda a: a.reshape(half, 2, width // units, a.shape[-1])
        k3, r3 = pair(keep3), pair(recv3)
        sx3, kx3 = add(k3[:, 1, :, :cut], r3[:, 1, :, :cut]), add(k3[:, 0, :, :cut], r3[:, 0, :, :cut])
        sy3, ky3 = add(k3[1, :, :, cut:], r3[1, :, :, cut:]), add(k3[0, :, :, cut:], r3[0, :, :, cut:])
        rx3 = swap(sx3, X_BIT)
        ry3 = swap(sy3, Y_BIT)
        gtwo = hop_two(gone)
        layer_out = jnp.stack([tie(outs[0], sx3), *outs[1:]])
        sxy, kxy = halve(tie(rx3, layer_out, *gtwo), kx3)
        rxy = swap(sxy, Y_BIT)
        syx, kyx = halve(tie(ry3, *gtwo), ky3)
        ryx = swap(syx, X_BIT)
        sz1, kz1 = halve_z0(tie(ry1, sxy, syx), ky1)
        rz1 = swap(sz1, 1)
        sz2, kz2 = halve_z0(tie(ry2, sxy, syx), ky2)
        rz2 = swap(sz2, 1)
        gparts = [tie(gsum, sz1, sz2), *gone, *gtwo]
    else:
        parts = token_grad(gf, dq_t, w_qkv)
        gparts = [lax.psum(gsum, "seq")]

    grad_tokens, gproj = last(gparts, parts, jnp.stack([p[2] for p in prepped]), jnp.stack([p[1] for p in prepped]), tokens)
    if not fast:
        layer_out = jnp.stack(outs)

    if not fast:
        g3 = jnp.stack(rest_grad(me, att, gfl, tok_t, dq_t, tt, gs_t, 0, stats), 1).reshape(width, -1)
        g2 = jnp.stack([in_grad(mt, dh, 0)[0], half2], 1).reshape(width, -1)
        g1 = jnp.stack([down_grad(at, gb, c) for c in (0, 1)], 1).reshape(ff, width)
        st = total(stat)
        st_in, st_qkv = gbin[0], jnp.sum(col, 0).reshape(-1)
        grads = (g3[:, width : 4 * width], st_qkv, g3[:, :width], st[5], st[3], st[4], g2, st_in, g1, st[2], st[0], st[1])
        grads = lax.psum_scatter(tuple(g.astype(F32) for g in grads), ("dp", "seq"), scatter_dimension=0, tiled=True)
        gproj = lax.psum(gproj, "dp").astype(F32)
        return (layer_out, grad_tokens, *grads, gproj)

    gproj = add(gproj, swap(gproj, CORE))
    sz3, kz3 = halve_rest(z0.reshape(1), kxy, rxy, kyx, ryx)
    rz3 = swap(sz3, 1)
    gproj = add(gproj, swap(gproj, X_BIT))
    gall = [gproj, swap(gproj, Y_BIT)]
    sw1, kw1 = halve_z1(rz1, kz1)
    rw1 = swap(sw1, 2)
    sw2, kw2 = halve_z1(rz2, kz2)
    rw2 = swap(sw2, 2)
    gproj = total([g.astype(F32) for g in gall])
    g1 = kw1.astype(F32) + rw1.astype(F32)
    g2 = kw2.astype(F32) + rw2.astype(F32)
    sw3, kw3 = halve_z1(rz3, kz3)
    rw3 = swap(sw3, 2)
    g_qkv, g_out, *small = finish_rest(z1.reshape(1), kw3, rw3)
    g_g2, g_b2, gb_down, g_g1, g_b1, gb_out, _, _, gb_qkv, gb_in = small
    return (
        layer_out, grad_tokens, g_qkv, gb_qkv, g_out, gb_out, g_g1, g_b1,
        g2, gb_in, g1, gb_down, g_g2, g_b2, gproj,
    )


def solution(mesh):
    both = ("dp", "seq")
    placed = (
        P("dp", "seq", None),
        P("dp", "seq"),
        P("dp", None, None),
        *([P()] * 12),
        P(None, "seq"),
        P("dp", "seq", None),
    )
    out = (
        P("dp", "seq", None),
        P("dp", "seq", None),
        P(both, None),
        P(both),
        P(both, None),
        P(both),
        P(both),
        P(both),
        P(both, None),
        P(both),
        P(both, None),
        P(both),
        P(both),
        P(both),
        P(None, "seq"),
    )
    run = functools.partial(body, mesh.shape["dp"], mesh.shape["seq"])
    return jax.shard_map(run, mesh=mesh, in_specs=placed, out_specs=out, check_vma=False)
```

profile of v0, /device:TPU:0, one launch (start us, length us, event | category | flops | bytes accessed | tf_op | source)
XLA Modules:
  0.0 227.5 jit_solution(6746683361633971735)
XLA Ops:
  0.7 2.7 %prep.2 = (bf16[272,768]{1,0:T(8,128)(2,1)}, bf16[256,512]{1,0:T(8,128)(2,1)}, bf16[256,512]{1,0:T(8,128)(2,1)}) custom-call(bf16[2,512,768]{2,1,0:T(8,128)(2,1)} %refs_8_.1, s32[2,512]{1,0:T(2,128)} %seg_ref.3, s32[2,4,256]{2,1,0:T(4,128)} %mask_ref.3, bf16[256,512]{1,0:T(8,128)(2,1)} %proj_ref.3), custom_call_target="tpu_custom_call" | custom-call | flops 201326592 | bytes 786432 | tf_op jit(solution)/shard_map/prep/pallas_call | solution.py:54
  3.4 3.0 %collective-permute-start = (bf16[272,768]{1,0:T(8,128)(2,1)}, bf16[272,768]{1,0:T(8,128)(2,1)}, u32[]{:S(2)}, u32[]{:S(2)}) collective-permute-start(bf16[272,768]{1,0:T(8,128)(2,1)} %get-tuple-element.109.refs_0_), channel_id=1, source_target_pairs={{0,1},{1,0},{2,3},{3,2},{4,5},{5,4},{6,7},{7,6},{8,9},{9,8},{10,11... | collective-permute-start | bytes 1253384 | tf_op jit(solution)/shard_map/ppermute | solution.py:951
  6.4 1.4 collective-permute-start.1
  8.6 2.6 %prep.3 = (bf16[272,768]{1,0:T(8,128)(2,1)}, bf16[256,512]{1,0:T(8,128)(2,1)}, bf16[256,512]{1,0:T(8,128)(2,1)}) custom-call(bf16[2,512,768]{2,1,0:T(8,128)(2,1)} %refs_8_.1, s32[2,512]{1,0:T(2,128)} %seg_ref.3, s32[2,4,256]{2,1,0:T(4,128)} %mask_ref.3, bf16[256,512]{1,0:T(8,128)(2,1)} %proj_ref.3), custom_call_target="tpu_custom_call" | custom-call | flops 201326592 | bytes 786432 | tf_op jit(solution)/shard_map/prep/pallas_call | solution.py:54
  11.8 2.7 %flip.1 = (bf16[2,768,768]{2,1,0:T(8,128)(2,1)S(1)}, f32[1536,1]{1,0:T(8,128)S(1)}, f32[3072,1]{1,0:T(8,128)S(1)}) custom-call(bf16[768,2304]{1,0:T(8,128)(2,1)} %refs_3_.1, f32[1,2304]{1,0:T(1,128)} %reshape.196.b_ref.bq_ref, f32[1,3072]{1,0:T(1,128)} %bitcast.111), custom_call_target="tpu_custom_call" | custom-call | bytes 4718592 | tf_op jit(solution)/shard_map/flip/pallas_call | solution.py:54
  14.5 1.1 copy-done.7
  16.4 1.4 collective-permute-start.3
  17.8 3.9 %collective-permute-start.2 = (bf16[272,768]{1,0:T(8,128)(2,1)}, bf16[272,768]{1,0:T(8,128)(2,1)}, u32[]{:S(2)}, u32[]{:S(2)}) collective-permute-start(bf16[272,768]{1,0:T(8,128)(2,1)} %collective-permute-done.1.refs_2_), channel_id=1, source_target_pairs={{0,1},{1,0},{2,3},{3,2},{4,5},{5,4},{6,7},{7,6},{8,9},{9,8},{10,11... | collective-permute-start | bytes 1253384 | tf_op jit(solution)/shard_map/ppermute | solution.py:954
  21.7 7.9 %query.1 = (bf16[2,768,512]{2,1,0:T(8,128)(2,1)}, bf16[2,4,2,96,512]{4,3,2,1,0:T(8,128)(2,1)}, bf16[768,3072]{1,0:T(8,128)(2,1)S(1)}, bf16[3072,768]{1,0:T(8,128)(2,1)S(1)}, bf16[768,768]{1,0:T(8,128)(2,1)S(1)}) custom-call(s32[1]{0:T(128)} %bitcast.me_ref, bf16[2,512,768]{2,1,0:T(8,128)(2,1)} %refs_8_.1, bf16[768,2304]{1,0:T(8,128)(2,1)} %refs_3_.1, ...), custom_call_target="tpu_custom_call" | custom-call | flops 1207959552 | bytes 4718592 | tf_op jit(solution)/shard_map/query/pallas_call | solution.py:54
  31.1 10.6 %attend.2 = (bf16[4,2,96,256]{3,2,1,0:T(8,128)(2,1)S(1)}, bf16[8,256]{1,0:T(8,128)(2,1)S(1)}, bf16[1536,256]{1,0:T(8,128)(2,1)S(1)}, bf16[12,256,512]{2,1,0:T(8,...) custom-call(s32[1]{0:T(128)} %bitcast.me_ref, ...), custom_call_target="tpu_custom_call" | custom-call | flops 2013265920 | bytes 10485760 | tf_op jit(solution)/shard_map/attend/pallas_call | solution.py:54
  41.6 4.2 %collective-permute-start.6 = (bf16[272,768]{1,0:T(8,128)(2,1)S(1)}, bf16[272,768]{1,0:T(8,128)(2,1)S(1)}, u32[]{:S(2)}, u32[]{:S(2)}) collective-permute-start(bf16[272,768]{1,0:T(8,128)(2,1)S(1)} %collective-permute-done.5.refs_2_), channel_id=1, source_target_pairs={{0,1},{1,0},{2,3},{3,2},{4,5},{5,4},{6,7},{7,6},{8,9},{9,8},{10,11... | collective-permute-start | bytes 1253384 | tf_op jit(solution)/shard_map/ppermute | solution.py:954
  46.8 20.9 %feed.2 = (bf16[4,2,96,512]{3,2,1,0:T(8,128)(2,1)S(1)}, bf16[4,2,384,512]{3,2,1,0:T(8,128)(2,1)S(1)}, bf16[512,768]{1,0:T(8,128)(2,1)S(1)}, bf16[3072,512]{1,0:T...) custom-call(s32[1]{0:T(128)} %bitcast.me_ref, ...), custom_call_target="tpu_custom_call" | custom-call | flops 9663676416 | bytes 25165824 | tf_op jit(solution)/shard_map/feed/pallas_call | solution.py:54
  67.7 10.3 %attend.3 = (bf16[4,2,96,256]{3,2,1,0:T(8,128)(2,1)S(1)}, bf16[8,256]{1,0:T(8,128)(2,1)S(1)}, bf16[1536,256]{1,0:T(8,128)(2,1)S(1)}, bf16[12,256,512]{2,1,0:T(8,...) custom-call(s32[1]{0:T(128)} %bitcast.me_ref, ...), custom_call_target="tpu_custom_call" | custom-call | flops 2013265920 | bytes 10485760 | tf_op jit(solution)/shard_map/attend/pallas_call | solution.py:54
  78.0 20.9 %feed.3 = (bf16[4,2,96,512]{3,2,1,0:T(8,128)(2,1)S(1)}, bf16[4,2,384,512]{3,2,1,0:T(8,128)(2,1)S(1)}, bf16[512,768]{1,0:T(8,128)(2,1)S(1)}, bf16[3072,512]{1,0:T...) custom-call(s32[1]{0:T(128)} %bitcast.me_ref, ...), custom_call_target="tpu_custom_call" | custom-call | flops 9663676416 | bytes 25165824 | tf_op jit(solution)/shard_map/feed/pallas_call | solution.py:54
  98.9 4.0 %down_grad.2 = bf16[4,384,768]{2,1,0:T(8,128)(2,1)} custom-call(bf16[4,2,384,512]{3,2,1,0:T(8,128)(2,1)S(1)} %get-tuple-element.147.refs_0_, bf16[4,2,384,512]{3,2,1,0:T(8,128)(2,1)S(1)} %get-tuple-element.139.refs_1_, bf16[512,768]{1,0:T(8,128)(2,1)S(1)} %get-tuple-element.140.refs_2_, bf16[512,768]{1,0:T(8,128)(2,1)S(1)} %get-tuple-element.141.refs_3_), custom_call_target="tpu_custom_call" | custom-call | flops 2415919104 | bytes 3145728 | tf_op jit(solution)/shard_map/down_grad/pallas_call | solution.py:54
  102.9 4.1 %in_grad.2 = (bf16[4,96,3072]{2,1,0:T(8,128)(2,1)}, f32[8,3072]{1,0:T(8,128)}) custom-call(bf16[4,2,96,512]{3,2,1,0:T(8,128)(2,1)S(1)} %get-tuple-element.152.refs_0_, bf16[4,2,96,512]{3,2,1,0:T(8,128)(2,1)S(1)} %get-tuple-element.143.refs_1_, bf16[3072,512]{1,0:T(8,128)(2,1)S(1)} %get-tuple-element.144.refs_2_, bf16[3072,512]{1,0:T(8,128)(2,1)S(1)} %get-tuple-element.145.refs_3_), custom_call_target="tpu_custom_call" | custom-call | flops 2415919104 | bytes 3145728 | tf_op jit(solution)/shard_map/in_grad/pallas_call | solution.py:54
  107.7 4.1 %down_grad.3 = (bf16[2,384,768]{2,1,0:T(8,128)(2,1)}, bf16[2,384,768]{2,1,0:T(8,128)(2,1)}) custom-call(bf16[4,2,384,512]{3,2,1,0:T(8,128)(2,1)S(1)} %get-tuple-element.147.refs_0_, bf16[4,2,384,512]{3,2,1,0:T(8,128)(2,1)S(1)} %get-tuple-element.139.refs_1_, bf16[512,768]{1,0:T(8,128)(2,1)S(1)} %get-tuple-element.140.refs_2_, ...), custom_call_target="tpu_custom_call" | custom-call | flops 2415919104 | bytes 3145728 | tf_op jit(solution)/shard_map/down_grad/pallas_call | solution.py:54
  111.9 4.1 %in_grad.3 = (bf16[2,96,3072]{2,1,0:T(8,128)(2,1)}, bf16[2,96,3072]{2,1,0:T(8,128)(2,1)}) custom-call(bf16[4,2,96,512]{3,2,1,0:T(8,128)(2,1)S(1)} %get-tuple-element.152.refs_0_, bf16[4,2,96,512]{3,2,1,0:T(8,128)(2,1)S(1)} %get-tuple-element.143.refs_1_, bf16[3072,512]{1,0:T(8,128)(2,1)S(1)} %get-tuple-element.144.refs_2_, ...), custom_call_target="tpu_custom_call" | custom-call | flops 2415919104 | bytes 3145728 | tf_op jit(solution)/shard_map/in_grad/pallas_call | solution.py:54
  116.0 1.5 collective-permute-start.11
  117.5 1.5 collective-permute-start.9
  119.7 15.6 %attend_back.1 = (bf16[2,768,512]{2,1,0:T(8,128)(2,1)S(1)}, bf16[2,1536,256]{2,1,0:T(8,128)(2,1)S(1)}, bf16[2,272,768]{2,1,0:T(8,128)(2,1)}, f32[2,2304,1]{2,1,0:T(8,128)S(1)}) custom-call(bf16[512,768]{1,0:T(8,128)(2,1)S(1)} %copy-done.2, bf16[512,768]{1,0:T(8,128)(2,1)S(1)} %copy-done.3, bf16[1536,256]{1,0:T(8,128)(2,1)S(1)} %get-tuple-element.156.refs_2_, ...), custom_call_target="tpu_custom_call" | custom-call | flops 2752512 | bytes 1024 | tf_op jit(solution)/shard_map/attend_back/pallas_call | solution.py:54
  135.3 1.7 collective-permute-start.14
  138.0 5.4 %token_grad.1.refs_5_ = f32[2,512,768]{2,1,0:T(8,128)} custom-call(f32[512,768]{1,0:T(8,128)} %get-tuple-element.150.refs_0_, f32[512,768]{1,0:T(8,128)} %get-tuple-element.151.refs_1_, bf16[2,768,512]{2,1,0:T(8,128)(2,1)S(1)} %get-tuple-element.162.refs_2_.refs_8_, bf16[768,2304]{1,0:T(8,128)(2,1)} %refs_3_.1), custom_call_target="tpu_custom_call" | custom-call | flops 589824 | bytes 1024 | tf_op jit(solution)/shard_map/token_grad/pallas_call | solution.py:54
  143.3 1.1 collective-permute-done.11
  145.9 1.6 collective-permute-start.13
  148.3 8.0 %rest_grad.1 = (bf16[4,96,3200]{2,1,0:T(8,128)(2,1)}, bf16[4,96,3200]{2,1,0:T(8,128)(2,1)}) custom-call(s32[1]{0:T(128)} %bitcast.me_ref, bf16[4,2,96,512]{3,2,1,0:T(8,128)(2,1)S(1)} %get-tuple-element.167.refs_0_, bf16[4,2,96,512]{3,2,1,0:T(8,128)(2,1)S(1)} %get-tuple-element.168.refs_1_, bf16[512,768]{1,0:T(8,128)(2,1)} %get-tuple-element.154.refs_0_.refs_2_, ...), custom_call_target="tpu_custom_call" | custom-call | flops 3538944 | bytes 1024 | tf_op jit(solution)/shard_map/rest_grad/pallas_call | solution.py:54
  156.3 4.1 %collective-permute-done.13 = bf16[96,3072]{1,0:T(8,128)(2,1)S(1)} collective-permute-done((bf16[96,3072]{1,0:T(8,128)(2,1)S(1)}, bf16[96,3072]{1,0:T(8,128)(2,1)S(1)}, u32[]{:S(2)}, u32[]{:S(2)}) %collective-permute-start.13) | collective-permute-done | bytes 589856 | tf_op jit(solution)/shard_map/ppermute | solution.py:945
  160.4 1.6 collective-permute-done.12
  162.0 1.6 collective-permute-start.18
  164.3 2.7 %collective-permute-done.16 = bf16[4,96,3200]{2,1,0:T(8,128)(2,1)} collective-permute-done((bf16[4,96,3200]{2,1,0:T(8,128)(2,1)}, bf16[4,96,3200]{2,1,0:T(8,128)(2,1)}, u32[]{:S(2)}, u32[]{:S(2)}) %collective-permute-start.16) | collective-permute-done | bytes 2457632 | tf_op jit(solution)/shard_map/ppermute | solution.py:945
  167.0 2.0 fusion
  169.0 1.5 fusion.5
  171.4 1.1 collective-permute-start.17
  172.5 1.4 add_convert_fusion.3
  173.9 1.3 pad_maximum_fusion
  175.2 7.8 %collective-permute-done.18.refs_3_ = bf16[2,272,768]{2,1,0:T(8,128)(2,1)S(1)} collective-permute-done((bf16[2,272,768]{2,1,0:T(8,128)(2,1)S(1)}, bf16[2,272,768]{2,1,0:T(8,128)(2,1)S(1)}, u32[]{:S(2)}, u32[]{:S(2)}) %collective-permute-start.18) | collective-permute-done | bytes 835616 | tf_op jit(solution)/shard_map/ppermute | solution.py:954
  183.0 3.5 %collective-permute-done.17 = bf16[2,96,1536]{2,1,0:T(8,128)(2,1)S(1)} collective-permute-done((bf16[2,96,1536]{2,1,0:T(8,128)(2,1)S(1)}, bf16[2,96,1536]{2,1,0:T(8,128)(2,1)S(1)}, u32[]{:S(2)}, u32[]{:S(2)}) %collective-permute-start.17) | collective-permute-done | bytes 589856 | tf_op jit(solution)/shard_map/ppermute | solution.py:945
  187.4 1.7 collective-permute-start.25
  189.1 1.1 pad_maximum_fusion.1
  192.0 1.1 collective-permute-start.22
  193.1 4.7 %last.1 = (f32[2,512,768]{2,1,0:T(8,128)}, bf16[256,512]{1,0:T(8,128)(2,1)}) custom-call(bf16[2,272,768]{2,1,0:T(8,128)(2,1)S(1)} %copy-done.4, bf16[2,272,768]{2,1,0:T(8,128)(2,1)S(1)} %collective-permute-done.14.refs_1_, bf16[2,272,768]{2,1,0:T(8,128)(2,1)S(1)} %collective-permute-done.15.refs_2_, ...), custom_call_target="tpu_custom_call" | custom-call | flops 805306368 | bytes 8388608 | tf_op jit(solution)/shard_map/last/pallas_call | solution.py:54
  197.9 2.5 %collective-permute-start.26 = (bf16[24,3072]{1,0:T(8,128)(2,1)S(1)}, bf16[24,3072]{1,0:T(8,128)(2,1)S(1)}, u32[]{:S(2)}, u32[]{:S(2)}) collective-permute-start(bf16[24,3072]{1,0:T(8,128)(2,1)S(1)} %fusion.19), channel_id=1, source_target_pairs={{0,2},{1,3},{2,0},{3,1},{4,6},{5,7},{6,4},{7,5},{8,10},{9,11},{10,... | collective-permute-start | bytes 442376 | tf_op jit(solution)/shard_map/ppermute | solution.py:945
  202.4 3.8 %collective-permute-start.28 = (bf16[96,768]{1,0:T(8,128)(2,1)S(1)}, bf16[96,768]{1,0:T(8,128)(2,1)S(1)}, u32[]{:S(2)}, u32[]{:S(2)}) collective-permute-start(bf16[96,768]{1,0:T(8,128)(2,1)S(1)} %fusion.21), channel_id=1, source_target_pairs={{0,2},{1,3},{2,0},{3,1},{4,6},{5,7},{6,4},{7,5},{8,10},{9,11},{10,... | collective-permute-start | bytes 442376 | tf_op jit(solution)/shard_map/ppermute | solution.py:945
  207.1 4.7 %collective-permute-done.26 = bf16[24,3072]{1,0:T(8,128)(2,1)S(1)} collective-permute-done((bf16[24,3072]{1,0:T(8,128)(2,1)S(1)}, bf16[24,3072]{1,0:T(8,128)(2,1)S(1)}, u32[]{:S(2)}, u32[]{:S(2)}) %collective-permute-start.26) | collective-permute-done | bytes 147488 | tf_op jit(solution)/shard_map/ppermute | solution.py:945
  212.7 1.2 collective-permute-start.31
  214.0 4.0 %collective-permute-done.23 = bf16[2,24,3200]{2,1,0:T(8,128)(2,1)S(1)} collective-permute-done((bf16[2,24,3200]{2,1,0:T(8,128)(2,1)}, bf16[2,24,3200]{2,1,0:T(8,128)(2,1)S(1)}, u32[]{:S(2)}, u32[]{:S(2)}) %collective-permute-start.23) | collective-permute-done | bytes 307232 | tf_op jit(solution)/shard_map/ppermute | solution.py:945
  218.0 1.1 collective-permute-start.24
  219.9 5.9 %collective-permute-done.24.recv_ref = bf16[24,3200]{1,0:T(8,128)(2,1)S(1)} collective-permute-done((bf16[24,3200]{1,0:T(8,128)(2,1)S(1)}, bf16[24,3200]{1,0:T(8,128)(2,1)S(1)}, u32[]{:S(2)}, u32[]{:S(2)}) %collective-permute-start.24) | collective-permute-done | bytes 153632 | tf_op jit(solution)/shard_map/ppermute | solution.py:945
  (119 shorter events, 19.8 us)
Async XLA Ops:
  0.6 7.2 %copy-start.21 = (f32[768]{0:T(1024)S(1)}, f32[768]{0:T(1024)}, u32[]{:S(2)}) copy-start(f32[768]{0:T(1024)} %param.23) | copy-start | bytes 9220
  0.7 7.2 %copy-start.23 = (f32[768]{0:T(1024)S(1)}, f32[768]{0:T(1024)}, u32[]{:S(2)}) copy-start(f32[768]{0:T(1024)} %param.25) | copy-start | bytes 9220
  0.7 7.2 %copy-start.24 = (f32[768]{0:T(1024)S(1)}, f32[768]{0:T(1024)}, u32[]{:S(2)}) copy-start(f32[768]{0:T(1024)} %param.29) | copy-start | bytes 9220
  0.7 7.2 %copy-start.25 = (f32[768]{0:T(1024)S(1)}, f32[768]{0:T(1024)}, u32[]{:S(2)}) copy-start(f32[768]{0:T(1024)} %param.30) | copy-start | bytes 9220
  0.7 7.2 %copy-start.26 = (f32[768]{0:T(1024)S(1)}, f32[768]{0:T(1024)}, u32[]{:S(2)}) copy-start(f32[768]{0:T(1024)} %param.31) | copy-start | bytes 9220
  0.7 10.5 %copy-start.20 = (f32[2304]{0:T(1024)S(1)}, f32[2304]{0:T(1024)}, u32[]{:S(2)}) copy-start(f32[2304]{0:T(1024)} %param.21) | copy-start | bytes 27652
  3.4 13.0 %collective-permute-start = (bf16[272,768]{1,0:T(8,128)(2,1)}, bf16[272,768]{1,0:T(8,128)(2,1)}, u32[]{:S(2)}, u32[]{:S(2)}) collective-permute-start(bf16[272,768]{1,0:T(8,128)(2,1)} %get-tuple-element.109.refs_0_), channel_id=1, source_target_pairs={{0,1},{1,0},{2,3},{3,2},{4,5},{5,4},{6,7},{7,6},{8,9},{9,8},{10,11... | collective-permute-start | bytes 1253384 | tf_op jit(solution)/shard_map/ppermute | solution.py:951
  6.4 11.4 %collective-permute-start.1 = (bf16[272,768]{1,0:T(8,128)(2,1)}, bf16[272,768]{1,0:T(8,128)(2,1)}, u32[]{:S(2)}, u32[]{:S(2)}) collective-permute-start(bf16[272,768]{1,0:T(8,128)(2,1)} %get-tuple-element.109.refs_0_), channel_id=1, source_target_pairs={{1,2},{2,1},{5,6},{6,5},{9,10},{10,9},{13,14},{14,13},{17,18},{18,... | collective-permute-start | bytes 1253384 | tf_op jit(solution)/shard_map/ppermute | solution.py:951
  16.4 14.0 %collective-permute-start.3 = (bf16[272,768]{1,0:T(8,128)(2,1)}, bf16[272,768]{1,0:T(8,128)(2,1)}, u32[]{:S(2)}, u32[]{:S(2)}) collective-permute-start(bf16[272,768]{1,0:T(8,128)(2,1)} %collective-permute-done.refs_1_), channel_id=1, source_target_pairs={{1,2},{2,1},{5,6},{6,5},{9,10},{10,9},{13,14},{14,13},{17,18},{18,... | collective-permute-start | bytes 1253384 | tf_op jit(solution)/shard_map/ppermute | solution.py:954
  17.8 13.2 %collective-permute-start.2 = (bf16[272,768]{1,0:T(8,128)(2,1)}, bf16[272,768]{1,0:T(8,128)(2,1)}, u32[]{:S(2)}, u32[]{:S(2)}) collective-permute-start(bf16[272,768]{1,0:T(8,128)(2,1)} %collective-permute-done.1.refs_2_), channel_id=1, source_target_pairs={{0,1},{1,0},{2,3},{3,2},{4,5},{5,4},{6,7},{7,6},{8,9},{9,8},{10,11... | collective-permute-start | bytes 1253384 | tf_op jit(solution)/shard_map/ppermute | solution.py:954
  21.7 7.9 %copy-start.5 = (bf16[272,768]{1,0:T(8,128)(2,1)S(1)}, bf16[272,768]{1,0:T(8,128)(2,1)}, u32[]{:S(2)}) copy-start(bf16[272,768]{1,0:T(8,128)(2,1)} %get-tuple-element.135.refs_0_) | copy-start | bytes 1253380
  21.7 9.4 %copy-start.6 = (bf16[272,768]{1,0:T(8,128)(2,1)S(1)}, bf16[272,768]{1,0:T(8,128)(2,1)}, u32[]{:S(2)}) copy-start(bf16[272,768]{1,0:T(8,128)(2,1)} %get-tuple-element.109.refs_0_) | copy-start | bytes 1253380
  29.6 12.1 %collective-permute-start.4 = (bf16[272,768]{1,0:T(8,128)(2,1)S(1)}, bf16[272,768]{1,0:T(8,128)(2,1)S(1)}, u32[]{:S(2)}, u32[]{:S(2)}) collective-permute-start(bf16[272,768]{1,0:T(8,128)(2,1)S(1)} %copy-done.5), channel_id=1, source_target_pairs={{0,1},{1,0},{2,3},{3,2},{4,5},{5,4},{6,7},{7,6},{8,9},{9,8},{10,11... | collective-permute-start | bytes 1253384 | tf_op jit(solution)/shard_map/ppermute | solution.py:951
  29.7 12.0 %collective-permute-start.5 = (bf16[272,768]{1,0:T(8,128)(2,1)S(1)}, bf16[272,768]{1,0:T(8,128)(2,1)S(1)}, u32[]{:S(2)}, u32[]{:S(2)}) collective-permute-start(bf16[272,768]{1,0:T(8,128)(2,1)S(1)} %copy-done.5), channel_id=1, source_target_pairs={{1,2},{2,1},{5,6},{6,5},{9,10},{10,9},{13,14},{14,13},{17,18},{18,... | collective-permute-start | bytes 1253384 | tf_op jit(solution)/shard_map/ppermute | solution.py:951
  31.1 15.7 %copy-start.8 = (f32[3072,1]{1,0:T(8,128)S(1)}, f32[3072,1]{1,0:T(8,128)}, u32[]{:S(2)}) copy-start(f32[3072,1]{1,0:T(8,128)} %copy-done.7) | copy-start | bytes 36868
  41.6 26.1 %collective-permute-start.6 = (bf16[272,768]{1,0:T(8,128)(2,1)S(1)}, bf16[272,768]{1,0:T(8,128)(2,1)S(1)}, u32[]{:S(2)}, u32[]{:S(2)}) collective-permute-start(bf16[272,768]{1,0:T(8,128)(2,1)S(1)} %collective-permute-done.5.refs_2_), channel_id=1, source_target_pairs={{0,1},{1,0},{2,3},{3,2},{4,5},{5,4},{6,7},{7,6},{8,9},{9,8},{10,11... | collective-permute-start | bytes 1253384 | tf_op jit(solution)/shard_map/ppermute | solution.py:954
  45.9 21.8 %collective-permute-start.7 = (bf16[272,768]{1,0:T(8,128)(2,1)S(1)}, bf16[272,768]{1,0:T(8,128)(2,1)S(1)}, u32[]{:S(2)}, u32[]{:S(2)}) collective-permute-start(bf16[272,768]{1,0:T(8,128)(2,1)S(1)} %collective-permute-done.4.refs_1_), channel_id=1, source_target_pairs={{1,2},{2,1},{5,6},{6,5},{9,10},{10,9},{13,14},{14,13},{17,18},{18,... | collective-permute-start | bytes 1253384 | tf_op jit(solution)/shard_map/ppermute | solution.py:954
  102.9 4.7 %collective-permute-start.8 = (bf16[4,384,768]{2,1,0:T(8,128)(2,1)}, bf16[4,384,768]{2,1,0:T(8,128)(2,1)S(1)}, u32[]{:S(2)}, u32[]{:S(2)}) collective-permute-start(bf16[4,384,768]{2,1,0:T(8,128)(2,1)} %down_grad.2), channel_id=1, source_target_pairs={{0,4},{1,5},{2,6},{3,7},{4,0},{5,1},{6,2},{7,3},{8,12},{9,13},{10,... | collective-permute-start | bytes 7077896 | tf_op jit(solution)/shard_map/ppermute | solution.py:945
  107.0 4.9 %collective-permute-start.10 = (bf16[4,96,3072]{2,1,0:T(8,128)(2,1)}, bf16[4,96,3072]{2,1,0:T(8,128)(2,1)S(1)}, u32[]{:S(2)}, u32[]{:S(2)}) collective-permute-start(bf16[4,96,3072]{2,1,0:T(8,128)(2,1)} %get-tuple-element.146), channel_id=1, source_target_pairs={{0,4},{1,5},{2,6},{3,7},{4,0},{5,1},{6,2},{7,3},{8,12},{9,13},{10,... | collective-permute-start | bytes 7077896 | tf_op jit(solution)/shard_map/ppermute | solution.py:945
  111.7 7.9 %copy-start.2 = (bf16[512,768]{1,0:T(8,128)(2,1)S(1)}, bf16[512,768]{1,0:T(8,128)(2,1)}, u32[]{:S(2)}) copy-start(bf16[512,768]{1,0:T(8,128)(2,1)} %get-tuple-element.154.refs_0_.refs_2_) | copy-start | bytes 2359300
  111.7 7.9 %copy-start.3 = (bf16[512,768]{1,0:T(8,128)(2,1)S(1)}, bf16[512,768]{1,0:T(8,128)(2,1)}, u32[]{:S(2)}) copy-start(bf16[512,768]{1,0:T(8,128)(2,1)} %get-tuple-element.155.refs_1_.refs_3_) | copy-start | bytes 2359300
  111.9 7.8 %copy-start = (bf16[12,256,512]{2,1,0:T(8,128)(2,1)S(1)}, bf16[12,256,512]{2,1,0:T(8,128)(2,1)}, u32[]{:S(2)}) copy-start(bf16[12,256,512]{2,1,0:T(8,128)(2,1)} %get-tuple-element.158.refs_4_) | copy-start | bytes 9437188
  111.9 7.8 %copy-start.1 = (bf16[12,256,512]{2,1,0:T(8,128)(2,1)S(1)}, bf16[12,256,512]{2,1,0:T(8,128)(2,1)}, u32[]{:S(2)}) copy-start(bf16[12,256,512]{2,1,0:T(8,128)(2,1)} %get-tuple-element.159.refs_5_) | copy-start | bytes 9437188
  116.0 28.5 %collective-permute-start.11 = (bf16[2,96,3072]{2,1,0:T(8,128)(2,1)}, bf16[2,96,3072]{2,1,0:T(8,128)(2,1)S(1)}, u32[]{:S(2)}, u32[]{:S(2)}) collective-permute-start(bf16[2,96,3072]{2,1,0:T(8,128)(2,1)} %get-tuple-element.153), channel_id=1, source_target_pairs={{0,16},{1,17},{2,18},{3,19},{4,20},{5,21},{6,22},{7,23},{8,24},{9,... | collective-permute-start | bytes 3538952 | tf_op jit(solution)/shard_map/ppermute | solution.py:945
  117.5 28.0 %collective-permute-start.9 = (bf16[2,384,768]{2,1,0:T(8,128)(2,1)S(1)}, bf16[2,384,768]{2,1,0:T(8,128)(2,1)S(1)}, u32[]{:S(2)}, u32[]{:S(2)}) collective-permute-start(bf16[2,384,768]{2,1,0:T(8,128)(2,1)S(1)} %copy-done.27), channel_id=1, source_target_pairs={{0,8},{1,9},{2,10},{3,11},{4,12},{5,13},{6,14},{7,15},{8,0},{9,1},... | collective-permute-start | bytes 3538952 | tf_op jit(solution)/shard_map/ppermute | solution.py:945
  135.3 21.0 %collective-permute-start.14 = (bf16[2,272,768]{2,1,0:T(8,128)(2,1)}, bf16[2,272,768]{2,1,0:T(8,128)(2,1)S(1)}, u32[]{:S(2)}, u32[]{:S(2)}) collective-permute-start(bf16[2,272,768]{2,1,0:T(8,128)(2,1)} %get-tuple-element.186.refs_0_), channel_id=1, source_target_pairs={{0,1},{1,0},{2,3},{3,2},{4,5},{5,4},{6,7},{7,6},{8,9},{9,8},{10,11... | collective-permute-start | bytes 2506760 | tf_op jit(solution)/shard_map/ppermute | solution.py:951
  137.0 19.4 %collective-permute-start.15 = (bf16[2,272,768]{2,1,0:T(8,128)(2,1)}, bf16[2,272,768]{2,1,0:T(8,128)(2,1)S(1)}, u32[]{:S(2)}, u32[]{:S(2)}) collective-permute-start(bf16[2,272,768]{2,1,0:T(8,128)(2,1)} %get-tuple-element.186.refs_0_), channel_id=1, source_target_pairs={{1,2},{2,1},{5,6},{6,5},{9,10},{10,9},{13,14},{14,13},{17,18},{18,... | collective-permute-start | bytes 2506760 | tf_op jit(solution)/shard_map/ppermute | solution.py:951
  138.0 7.5 %copy-start.10 = (bf16[2,96,3072]{2,1,0:T(8,128)(2,1)S(1)}, bf16[2,96,3072]{2,1,0:T(8,128)(2,1)}, u32[]{:S(2)}) copy-start(bf16[2,96,3072]{2,1,0:T(8,128)(2,1)} %get-tuple-element.164) | copy-start | bytes 3538948
  145.9 14.5 %collective-permute-start.13 = (bf16[96,3072]{1,0:T(8,128)(2,1)S(1)}, bf16[96,3072]{1,0:T(8,128)(2,1)S(1)}, u32[]{:S(2)}, u32[]{:S(2)}) collective-permute-start(bf16[96,3072]{1,0:T(8,128)(2,1)S(1)} %get-tuple-element.206), channel_id=1, source_target_pairs={{0,8},{1,9},{2,10},{3,11},{4,12},{5,13},{6,14},{7,15},{8,0},{9,1},... | collective-permute-start | bytes 1769480 | tf_op jit(solution)/shard_map/ppermute | solution.py:945
  147.7 14.3 %collective-permute-start.12 = (bf16[384,768]{1,0:T(8,128)(2,1)S(1)}, bf16[384,768]{1,0:T(8,128)(2,1)S(1)}, u32[]{:S(2)}, u32[]{:S(2)}) collective-permute-start(bf16[384,768]{1,0:T(8,128)(2,1)S(1)} %get-tuple-element.208), channel_id=1, source_target_pairs={{0,16},{1,17},{2,18},{3,19},{4,20},{5,21},{6,22},{7,23},{8,24},{9,... | collective-permute-start | bytes 1769480 | tf_op jit(solution)/shard_map/ppermute | solution.py:945
  162.0 5.0 %collective-permute-start.16 = (bf16[4,96,3200]{2,1,0:T(8,128)(2,1)}, bf16[4,96,3200]{2,1,0:T(8,128)(2,1)}, u32[]{:S(2)}, u32[]{:S(2)}) collective-permute-start(bf16[4,96,3200]{2,1,0:T(8,128)(2,1)} %get-tuple-element.179), channel_id=1, source_target_pairs={{0,4},{1,5},{2,6},{3,7},{4,0},{5,1},{6,2},{7,3},{8,12},{9,13},{10,... | collective-permute-start | bytes 7372808 | tf_op jit(solution)/shard_map/ppermute | solution.py:945
  162.0 21.0 %collective-permute-start.18 = (bf16[2,272,768]{2,1,0:T(8,128)(2,1)S(1)}, bf16[2,272,768]{2,1,0:T(8,128)(2,1)S(1)}, u32[]{:S(2)}, u32[]{:S(2)}) collective-permute-start(bf16[2,272,768]{2,1,0:T(8,128)(2,1)S(1)} %collective-permute-done.15.refs_2_), channel_id=1, source_target_pairs={{0,1},{1,0},{2,3},{3,2},{4,5},{5,4},{6,7},{7,6},{8,9},{9,8},{10,11... | collective-permute-start | bytes 2506760 | tf_op jit(solution)/shard_map/ppermute | solution.py:954
  163.6 19.4 %collective-permute-start.19 = (bf16[2,272,768]{2,1,0:T(8,128)(2,1)S(1)}, bf16[2,272,768]{2,1,0:T(8,128)(2,1)S(1)}, u32[]{:S(2)}, u32[]{:S(2)}) collective-permute-start(bf16[2,272,768]{2,1,0:T(8,128)(2,1)S(1)} %collective-permute-done.14.refs_1_), channel_id=1, source_target_pairs={{1,2},{2,1},{5,6},{6,5},{9,10},{10,9},{13,14},{14,13},{17,18},{18,... | collective-permute-start | bytes 2506760 | tf_op jit(solution)/shard_map/ppermute | solution.py:954
  170.5 16.5 %collective-permute-start.20 = (bf16[2,96,1664]{2,1,0:T(8,128)(2,1)S(1)}, bf16[2,96,1664]{2,1,0:T(8,128)(2,1)S(1)}, u32[]{:S(2)}, u32[]{:S(2)}) collective-permute-start(bf16[2,96,1664]{2,1,0:T(8,128)(2,1)S(1)} %get-tuple-element.203), channel_id=1, source_target_pairs={{0,16},{1,17},{2,18},{3,19},{4,20},{5,21},{6,22},{7,23},{8,24},{9,... | collective-permute-start | bytes 1916936 | tf_op jit(solution)/shard_map/ppermute | solution.py:945
  171.4 15.1 %collective-permute-start.17 = (bf16[2,96,1536]{2,1,0:T(8,128)(2,1)S(1)}, bf16[2,96,1536]{2,1,0:T(8,128)(2,1)S(1)}, u32[]{:S(2)}, u32[]{:S(2)}) collective-permute-start(bf16[2,96,1536]{2,1,0:T(8,128)(2,1)S(1)} %fusion.5), channel_id=1, source_target_pairs={{0,8},{1,9},{2,10},{3,11},{4,12},{5,13},{6,14},{7,15},{8,0},{9,1},... | collective-permute-start | bytes 1769480 | tf_op jit(solution)/shard_map/ppermute | solution.py:945
  175.2 12.0 %copy-start.16 = (bf16[96,3072]{1,0:T(8,128)(2,1)S(1)}, bf16[96,3072]{1,0:T(8,128)(2,1)}, u32[]{:S(2)}) copy-start(bf16[96,3072]{1,0:T(8,128)(2,1)} %copy-done.15) | copy-start | bytes 1769476
  187.4 10.4 %collective-permute-start.25 = (bf16[2,24,3072]{2,1,0:T(8,128)(2,1)S(1)}, bf16[2,24,3072]{2,1,0:T(8,128)(2,1)S(1)}, u32[]{:S(2)}, u32[]{:S(2)}) collective-permute-start(bf16[2,24,3072]{2,1,0:T(8,128)(2,1)S(1)} %get-tuple-element.214), channel_id=1, source_target_pairs={{0,1},{1,0},{2,3},{3,2},{4,5},{5,4},{6,7},{7,6},{8,9},{9,8},{10,11... | collective-permute-start | bytes 884744 | tf_op jit(solution)/shard_map/ppermute | solution.py:945
  190.1 16.1 %collective-permute-start.21 = (bf16[96,1536]{1,0:T(8,128)(2,1)S(1)}, bf16[96,1536]{1,0:T(8,128)(2,1)S(1)}, u32[]{:S(2)}, u32[]{:S(2)}) collective-permute-start(bf16[96,1536]{1,0:T(8,128)(2,1)S(1)} %get-tuple-element.216), channel_id=1, source_target_pairs={{0,16},{1,17},{2,18},{3,19},{4,20},{5,21},{6,22},{7,23},{8,24},{9,... | collective-permute-start | bytes 884744 | tf_op jit(solution)/shard_map/ppermute | solution.py:945
  191.2 11.2 %collective-permute-start.27 = (bf16[2,96,768]{2,1,0:T(8,128)(2,1)S(1)}, bf16[2,96,768]{2,1,0:T(8,128)(2,1)S(1)}, u32[]{:S(2)}, u32[]{:S(2)}) collective-permute-start(bf16[2,96,768]{2,1,0:T(8,128)(2,1)S(1)} %get-tuple-element.212), channel_id=1, source_target_pairs={{0,1},{1,0},{2,3},{3,2},{4,5},{5,4},{6,7},{7,6},{8,9},{9,8},{10,11... | collective-permute-start | bytes 884744 | tf_op jit(solution)/shard_map/ppermute | solution.py:945
  192.0 14.2 %collective-permute-start.22 = (bf16[96,1664]{1,0:T(8,128)(2,1)S(1)}, bf16[96,1664]{1,0:T(8,128)(2,1)S(1)}, u32[]{:S(2)}, u32[]{:S(2)}) collective-permute-start(bf16[96,1664]{1,0:T(8,128)(2,1)S(1)} %get-tuple-element.210), channel_id=1, source_target_pairs={{0,8},{1,9},{2,10},{3,11},{4,12},{5,13},{6,14},{7,15},{8,0},{9,1},... | collective-permute-start | bytes 958472 | tf_op jit(solution)/shard_map/ppermute | solution.py:945
  197.8 2.5 %collective-permute-start.29 = (bf16[256,512]{1,0:T(8,128)(2,1)}, bf16[256,512]{1,0:T(8,128)(2,1)S(1)}, u32[]{:S(2)}, u32[]{:S(2)}) collective-permute-start(bf16[256,512]{1,0:T(8,128)(2,1)} %get-tuple-element.202), channel_id=1, source_target_pairs={{0,4},{1,5},{2,6},{3,7},{4,0},{5,1},{6,2},{7,3},{8,12},{9,13},{10,... | collective-permute-start | bytes 786440 | tf_op jit(solution)/shard_map/ppermute | solution.py:945
  197.9 14.0 %collective-permute-start.26 = (bf16[24,3072]{1,0:T(8,128)(2,1)S(1)}, bf16[24,3072]{1,0:T(8,128)(2,1)S(1)}, u32[]{:S(2)}, u32[]{:S(2)}) collective-permute-start(bf16[24,3072]{1,0:T(8,128)(2,1)S(1)} %fusion.19), channel_id=1, source_target_pairs={{0,2},{1,3},{2,0},{3,1},{4,6},{5,7},{6,4},{7,5},{8,10},{9,11},{10,... | collective-permute-start | bytes 442376 | tf_op jit(solution)/shard_map/ppermute | solution.py:945
  201.3 11.3 %collective-permute-start.30 = (bf16[256,512]{1,0:T(8,128)(2,1)S(1)}, bf16[256,512]{1,0:T(8,128)(2,1)S(1)}, u32[]{:S(2)}, u32[]{:S(2)}) collective-permute-start(bf16[256,512]{1,0:T(8,128)(2,1)S(1)} %add_convert_fusion.13), channel_id=1, source_target_pairs={{0,8},{1,9},{2,10},{3,11},{4,12},{5,13},{6,14},{7,15},{8,0},{9,1},... | collective-permute-start | bytes 786440 | tf_op jit(solution)/shard_map/ppermute | solution.py:945
  202.4 16.7 %collective-permute-start.28 = (bf16[96,768]{1,0:T(8,128)(2,1)S(1)}, bf16[96,768]{1,0:T(8,128)(2,1)S(1)}, u32[]{:S(2)}, u32[]{:S(2)}) collective-permute-start(bf16[96,768]{1,0:T(8,128)(2,1)S(1)} %fusion.21), channel_id=1, source_target_pairs={{0,2},{1,3},{2,0},{3,1},{4,6},{5,7},{6,4},{7,5},{8,10},{9,11},{10,... | collective-permute-start | bytes 442376 | tf_op jit(solution)/shard_map/ppermute | solution.py:945
  207.1 10.8 %copy-start.17 = (bf16[2,24,3200]{2,1,0:T(8,128)(2,1)S(1)}, bf16[2,24,3200]{2,1,0:T(8,128)(2,1)}, u32[]{:S(2)}) copy-start(bf16[2,24,3200]{2,1,0:T(8,128)(2,1)} %get-tuple-element.190) | copy-start | bytes 921604
  207.1 10.8 %collective-permute-start.23 = (bf16[2,24,3200]{2,1,0:T(8,128)(2,1)}, bf16[2,24,3200]{2,1,0:T(8,128)(2,1)S(1)}, u32[]{:S(2)}, u32[]{:S(2)}) collective-permute-start(bf16[2,24,3200]{2,1,0:T(8,128)(2,1)} %get-tuple-element.191), channel_id=1, source_target_pairs={{0,1},{1,0},{2,3},{3,2},{4,5},{5,4},{6,7},{7,6},{8,9},{9,8},{10,11... | collective-permute-start | bytes 921608 | tf_op jit(solution)/shard_map/ppermute | solution.py:945
  212.7 13.9 %collective-permute-start.31 = (bf16[256,512]{1,0:T(8,128)(2,1)S(1)}, bf16[256,512]{1,0:T(8,128)(2,1)S(1)}, u32[]{:S(2)}, u32[]{:S(2)}) collective-permute-start(bf16[256,512]{1,0:T(8,128)(2,1)S(1)} %add_convert_fusion.12), channel_id=1, source_target_pairs={{0,16},{1,17},{2,18},{3,19},{4,20},{5,21},{6,22},{7,23},{8,24},{9,... | collective-permute-start | bytes 786440 | tf_op jit(solution)/shard_map/ppermute | solution.py:945
  218.0 7.7 %collective-permute-start.24 = (bf16[24,3200]{1,0:T(8,128)(2,1)S(1)}, bf16[24,3200]{1,0:T(8,128)(2,1)S(1)}, u32[]{:S(2)}, u32[]{:S(2)}) collective-permute-start(bf16[24,3200]{1,0:T(8,128)(2,1)S(1)} %get-tuple-element.217), channel_id=1, source_target_pairs={{0,2},{1,3},{2,0},{3,1},{4,6},{5,7},{6,4},{7,5},{8,10},{9,11},{10,... | collective-permute-start | bytes 460808 | tf_op jit(solution)/shard_map/ppermute | solution.py:945
  (12 other events, 39.6 us)
where the time goes:
time: 228 us; the launch traced here: 227 us
  Pallas kernels  130 us (57%)
  starting transfers between devices  42.3 us (19%)
  waiting for transfers between devices  38.5 us (17%)
  other arithmetic  12.1 us (5%)
  local copies, waits for them, and re-layouts  3.12 us (1%)
    pallas_call x18, Pallas kernels, call(): pl.pallas_call(kernel, tuple(shapes), grid_spec=pltpu.PrefetchScalarGridS...  130 us
    ppermute x20, waiting for transfers between devices, swap(): return lax.ppermute(x, ('dp', 'seq'), pairs)  29.3 us
    ppermute x20, starting transfers between devices, swap(): return lax.ppermute(x, ('dp', 'seq'), pairs)  21.7 us
    ppermute x3, starting transfers between devices, hop_two(): lax.ppermute(first[1], 'seq', near)  9.72 us
    ppermute x3, waiting for transfers between devices, hop_two(): lax.ppermute(first[1], 'seq', near)  8.53 us
    ppermute x6, starting transfers between devices, hop_one(): return (lax.ppermute(own, 'seq', near), lax.ppermute(own, 'seq', mid))  7.87 us
    convert_element_type x14, other arithmetic, add(): return (a.astype(F32) + b.astype(F32)).astype(BF16)  7.37 us
  transfers between devices with their start and end apart: 32, of which 15 were waited for; matrix products, arithmetic and copies ran while one was open for 6% of the time, Pallas kernels for 39%

commit v1 on v0

--- a/solution.py
+++ b/solution.py
@@ -274,18 +274,19 @@
     lax.fori_loop(0, heads // GROUP, heads_of, 0)
     att = att_scr[...]
     res_scr[...] = dot(att, wo_ref[...], 0, 0)
+    block_rows = min(2 * LN_ROWS, length)
     for u in range(units):
         r = u ^ me
         att_ref[r >> 1, r & 1] = att_scr[u * rows : (u + 1) * rows, :]
 
     def tile(i, carry):
-        part = pl.ds(pl.multiple_of(i * LN_ROWS, LN_ROWS), LN_ROWS)
+        part = pl.ds(pl.multiple_of(i * block_rows, block_rows), block_rows)
         normed, inverse = norm_stats(res_scr[part, :] + tok_ref[0, part, :].astype(F32) + vec_ref[0:1, :])
         n_ref[part, :] = normed
         inv_ref[part, :] = inverse
         return carry
 
-    lax.fori_loop(0, length // LN_ROWS, tile, 0)
+    lax.fori_loop(0, length // block_rows, tile, 0)
     for g in range(heads // GROUP):
         store(g).wait()
 
@@ -588,8 +589,9 @@
     gt = dot(gs[0:width], wkv_ref[0], 0, 0) + dot(gs[width:], wkv_ref[1], 0, 0)
     gt_ref[0, 0:KP, :] = gt.astype(BF16)
     pad = TE - KP
-    b_hi = bkv_ref[...].astype(BF16)
-    b_lo = (bkv_ref[...] - b_hi.astype(F32)).astype(BF16)
+    b_kv = bkv_ref[:, width:]
+    b_hi = b_kv.astype(BF16)
+    b_lo = (b_kv - b_hi.astype(F32)).astype(BF16)
     drow = dot(jnp.broadcast_to(b_hi, (pad, 2 * width)), gs) + dot(jnp.broadcast_to(b_lo, (pad, 2 * width)), gs)
     gt_ref[0, KP:TE, :] = jnp.concatenate([drow.astype(BF16), jnp.zeros((pad, width - KP), BF16)], 1)
 
@@ -607,7 +609,7 @@
             (w_out, "v", None),
             (q_t, "h", None),
             (wkv_t, "v", None),
-            (bkv_row, "h", whole((1, 2 * width))),
+            (bkv_row, "h", whole((1, 3 * width))),
         ],
         [
             (V(seqs, width, length), None),
@@ -1016,7 +1018,7 @@
         rx2 = swap(sx2, Y_BIT)
         back_in[0] = tie(gfl[0], sx2)
 
-    dq_t, gs_t, gsum, col = attend_back(back_in, w_out, kv, probs, q_t, crow, wkv_t, row(b_qkv[width:]))
+    dq_t, gs_t, gsum, col = attend_back(back_in, w_out, kv, probs, q_t, crow, wkv_t, row(b_qkv))
     if not fast:
         half2, gbin = in_grad(mt, dh, 1)
     stats = (stat, gbin, col)

time: 228 us -> 228 us (level)
  transfers between devices with their start and end apart: 32 -> 32, of which waited for: 15 -> 15; matrix products, arithmetic and copies ran while one was open for 6% -> 5% of each run, Pallas kernels for 39% -> 39%
where the time goes in v1:
time: 228 us; the launch traced here: 227 us
  Pallas kernels  130 us (57%)
  starting transfers between devices  42.4 us (19%)
  waiting for transfers between devices  39.1 us (17%)
  other arithmetic  12.1 us (5%)
  local copies, waits for them, and re-layouts  2.51 us (1%)
    pallas_call x18, Pallas kernels, call(): pl.pallas_call(kernel, tuple(shapes), grid_spec=pltpu.PrefetchScalarGridS...  130 us
    ppermute x20, waiting for transfers between devices, swap(): return lax.ppermute(x, ('dp', 'seq'), pairs)  29.9 us
    ppermute x20, starting transfers between devices, swap(): return lax.ppermute(x, ('dp', 'seq'), pairs)  21.7 us
    ppermute x3, starting transfers between devices, hop_two(): lax.ppermute(first[1], 'seq', near)  9.75 us
    ppermute x3, waiting for transfers between devices, hop_two(): lax.ppermute(first[1], 'seq', near)  8.52 us
    ppermute x6, starting transfers between devices, hop_one(): return (lax.ppermute(own, 'seq', near), lax.ppermute(own, 'seq', mid))  7.88 us
    convert_element_type x14, other arithmetic, add(): return (a.astype(F32) + b.astype(F32)).astype(BF16)  7.37 us
  transfers between devices with their start and end apart: 32, of which 15 were waited for; matrix products, arithmetic and copies ran while one was open for 5% of the time, Pallas kernels for 39%

profile of v1, /device:TPU:0, one launch (start us, length us, event | category | flops | bytes accessed | tf_op | source)
XLA Modules:
  0.0 226.8 jit_solution(10238791536113361829)
XLA Ops:
  0.7 2.7 %prep.2 = (bf16[272,768]{1,0:T(8,128)(2,1)}, bf16[256,512]{1,0:T(8,128)(2,1)}, bf16[256,512]{1,0:T(8,128)(2,1)}) custom-call(bf16[2,512,768]{2,1,0:T(8,128)(2,1)} %refs_8_.1, s32[2,512]{1,0:T(2,128)} %seg_ref.3, s32[2,4,256]{2,1,0:T(4,128)} %mask_ref.3, bf16[256,512]{1,0:T(8,128)(2,1)} %proj_ref.3), custom_call_target="tpu_custom_call" | custom-call | flops 201326592 | bytes 786432 | tf_op jit(solution)/shard_map/prep/pallas_call | solution.py:54
  3.4 3.0 %collective-permute-start = (bf16[272,768]{1,0:T(8,128)(2,1)}, bf16[272,768]{1,0:T(8,128)(2,1)}, u32[]{:S(2)}, u32[]{:S(2)}) collective-permute-start(bf16[272,768]{1,0:T(8,128)(2,1)} %get-tuple-element.109.refs_0_), channel_id=1, source_target_pairs={{0,1},{1,0},{2,3},{3,2},{4,5},{5,4},{6,7},{7,6},{8,9},{9,8},{10,11... | collective-permute-start | bytes 1253384 | tf_op jit(solution)/shard_map/ppermute | solution.py:953
  6.4 1.4 collective-permute-start.1
  8.6 2.6 %prep.3 = (bf16[272,768]{1,0:T(8,128)(2,1)}, bf16[256,512]{1,0:T(8,128)(2,1)}, bf16[256,512]{1,0:T(8,128)(2,1)}) custom-call(bf16[2,512,768]{2,1,0:T(8,128)(2,1)} %refs_8_.1, s32[2,512]{1,0:T(2,128)} %seg_ref.3, s32[2,4,256]{2,1,0:T(4,128)} %mask_ref.3, bf16[256,512]{1,0:T(8,128)(2,1)} %proj_ref.3), custom_call_target="tpu_custom_call" | custom-call | flops 201326592 | bytes 786432 | tf_op jit(solution)/shard_map/prep/pallas_call | solution.py:54
  11.8 2.7 %flip.1 = (bf16[2,768,768]{2,1,0:T(8,128)(2,1)S(1)}, f32[1536,1]{1,0:T(8,128)S(1)}, f32[3072,1]{1,0:T(8,128)S(1)}) custom-call(bf16[768,2304]{1,0:T(8,128)(2,1)} %refs_3_.1, f32[1,2304]{1,0:T(1,128)} %reshape.194.b_ref.bq_ref.refs_11_, f32[1,3072]{1,0:T(1,128)} %bitcast.111), custom_call_target="tpu_custom_call" | custom-call | bytes 4718592 | tf_op jit(solution)/shard_map/flip/pallas_call | solution.py:54
  14.5 1.1 copy-done.7
  16.4 1.4 collective-permute-start.3
  17.8 3.9 %collective-permute-start.2 = (bf16[272,768]{1,0:T(8,128)(2,1)}, bf16[272,768]{1,0:T(8,128)(2,1)}, u32[]{:S(2)}, u32[]{:S(2)}) collective-permute-start(bf16[272,768]{1,0:T(8,128)(2,1)} %collective-permute-done.1.refs_2_), channel_id=1, source_target_pairs={{0,1},{1,0},{2,3},{3,2},{4,5},{5,4},{6,7},{7,6},{8,9},{9,8},{10,11... | collective-permute-start | bytes 1253384 | tf_op jit(solution)/shard_map/ppermute | solution.py:956
  21.7 7.9 %query.1 = (bf16[2,768,512]{2,1,0:T(8,128)(2,1)}, bf16[2,4,2,96,512]{4,3,2,1,0:T(8,128)(2,1)}, bf16[768,3072]{1,0:T(8,128)(2,1)S(1)}, bf16[3072,768]{1,0:T(8,128)(2,1)S(1)}, bf16[768,768]{1,0:T(8,128)(2,1)S(1)}) custom-call(s32[1]{0:T(128)} %bitcast.me_ref, bf16[2,512,768]{2,1,0:T(8,128)(2,1)} %refs_8_.1, bf16[768,2304]{1,0:T(8,128)(2,1)} %refs_3_.1, ...), custom_call_target="tpu_custom_call" | custom-call | flops 1207959552 | bytes 4718592 | tf_op jit(solution)/shard_map/query/pallas_call | solution.py:54
  31.1 10.2 %attend.2 = (bf16[4,2,96,256]{3,2,1,0:T(8,128)(2,1)S(1)}, bf16[8,256]{1,0:T(8,128)(2,1)S(1)}, bf16[1536,256]{1,0:T(8,128)(2,1)S(1)}, bf16[12,256,512]{2,1,0:T(8,...) custom-call(s32[1]{0:T(128)} %bitcast.me_ref, ...), custom_call_target="tpu_custom_call" | custom-call | flops 2013265920 | bytes 10485760 | tf_op jit(solution)/shard_map/attend/pallas_call | solution.py:54
  41.3 4.3 %collective-permute-start.6 = (bf16[272,768]{1,0:T(8,128)(2,1)S(1)}, bf16[272,768]{1,0:T(8,128)(2,1)S(1)}, u32[]{:S(2)}, u32[]{:S(2)}) collective-permute-start(bf16[272,768]{1,0:T(8,128)(2,1)S(1)} %collective-permute-done.5.refs_2_), channel_id=1, source_target_pairs={{0,1},{1,0},{2,3},{3,2},{4,5},{5,4},{6,7},{7,6},{8,9},{9,8},{10,11... | collective-permute-start | bytes 1253384 | tf_op jit(solution)/shard_map/ppermute | solution.py:956
  46.4 20.9 %feed.2 = (bf16[4,2,96,512]{3,2,1,0:T(8,128)(2,1)S(1)}, bf16[4,2,384,512]{3,2,1,0:T(8,128)(2,1)S(1)}, bf16[512,768]{1,0:T(8,128)(2,1)S(1)}, bf16[3072,512]{1,0:T...) custom-call(s32[1]{0:T(128)} %bitcast.me_ref, ...), custom_call_target="tpu_custom_call" | custom-call | flops 9663676416 | bytes 25165824 | tf_op jit(solution)/shard_map/feed/pallas_call | solution.py:54
  67.4 9.9 %attend.3 = (bf16[4,2,96,256]{3,2,1,0:T(8,128)(2,1)S(1)}, bf16[8,256]{1,0:T(8,128)(2,1)S(1)}, bf16[1536,256]{1,0:T(8,128)(2,1)S(1)}, bf16[12,256,512]{2,1,0:T(8,...) custom-call(s32[1]{0:T(128)} %bitcast.me_ref, ...), custom_call_target="tpu_custom_call" | custom-call | flops 2013265920 | bytes 10485760 | tf_op jit(solution)/shard_map/attend/pallas_call | solution.py:54
  77.3 20.9 %feed.3 = (bf16[4,2,96,512]{3,2,1,0:T(8,128)(2,1)S(1)}, bf16[4,2,384,512]{3,2,1,0:T(8,128)(2,1)S(1)}, bf16[512,768]{1,0:T(8,128)(2,1)S(1)}, bf16[3072,512]{1,0:T...) custom-call(s32[1]{0:T(128)} %bitcast.me_ref, ...), custom_call_target="tpu_custom_call" | custom-call | flops 9663676416 | bytes 25165824 | tf_op jit(solution)/shard_map/feed/pallas_call | solution.py:54
  98.2 4.0 %down_grad.2 = bf16[4,384,768]{2,1,0:T(8,128)(2,1)} custom-call(bf16[4,2,384,512]{3,2,1,0:T(8,128)(2,1)S(1)} %get-tuple-element.147.refs_0_, bf16[4,2,384,512]{3,2,1,0:T(8,128)(2,1)S(1)} %get-tuple-element.139.refs_1_, bf16[512,768]{1,0:T(8,128)(2,1)S(1)} %get-tuple-element.140.refs_2_, bf16[512,768]{1,0:T(8,128)(2,1)S(1)} %get-tuple-element.141.refs_3_), custom_call_target="tpu_custom_call" | custom-call | flops 2415919104 | bytes 3145728 | tf_op jit(solution)/shard_map/down_grad/pallas_call | solution.py:54
  102.2 4.1 %in_grad.2 = (bf16[4,96,3072]{2,1,0:T(8,128)(2,1)}, f32[8,3072]{1,0:T(8,128)}) custom-call(bf16[4,2,96,512]{3,2,1,0:T(8,128)(2,1)S(1)} %get-tuple-element.152.refs_0_, bf16[4,2,96,512]{3,2,1,0:T(8,128)(2,1)S(1)} %get-tuple-element.143.refs_1_, bf16[3072,512]{1,0:T(8,128)(2,1)S(1)} %get-tuple-element.144.refs_2_, bf16[3072,512]{1,0:T(8,128)(2,1)S(1)} %get-tuple-element.145.refs_3_), custom_call_target="tpu_custom_call" | custom-call | flops 2415919104 | bytes 3145728 | tf_op jit(solution)/shard_map/in_grad/pallas_call | solution.py:54
  107.0 4.1 %down_grad.3 = (bf16[2,384,768]{2,1,0:T(8,128)(2,1)}, bf16[2,384,768]{2,1,0:T(8,128)(2,1)}) custom-call(bf16[4,2,384,512]{3,2,1,0:T(8,128)(2,1)S(1)} %get-tuple-element.147.refs_0_, bf16[4,2,384,512]{3,2,1,0:T(8,128)(2,1)S(1)} %get-tuple-element.139.refs_1_, bf16[512,768]{1,0:T(8,128)(2,1)S(1)} %get-tuple-element.140.refs_2_, ...), custom_call_target="tpu_custom_call" | custom-call | flops 2415919104 | bytes 3145728 | tf_op jit(solution)/shard_map/down_grad/pallas_call | solution.py:54
  111.2 4.1 %in_grad.3 = (bf16[2,96,3072]{2,1,0:T(8,128)(2,1)}, bf16[2,96,3072]{2,1,0:T(8,128)(2,1)}) custom-call(bf16[4,2,96,512]{3,2,1,0:T(8,128)(2,1)S(1)} %get-tuple-element.152.refs_0_, bf16[4,2,96,512]{3,2,1,0:T(8,128)(2,1)S(1)} %get-tuple-element.143.refs_1_, bf16[3072,512]{1,0:T(8,128)(2,1)S(1)} %get-tuple-element.144.refs_2_, ...), custom_call_target="tpu_custom_call" | custom-call | flops 2415919104 | bytes 3145728 | tf_op jit(solution)/shard_map/in_grad/pallas_call | solution.py:54
  115.3 1.5 collective-permute-start.11
  116.8 1.5 collective-permute-start.9
  118.3 15.6 %attend_back.1 = (bf16[2,768,512]{2,1,0:T(8,128)(2,1)S(1)}, bf16[2,1536,256]{2,1,0:T(8,128)(2,1)S(1)}, bf16[2,272,768]{2,1,0:T(8,128)(2,1)}, f32[2,2304,1]{2,1,0:T(8,128)S(1)}) custom-call(bf16[512,768]{1,0:T(8,128)(2,1)S(1)} %copy-done, bf16[512,768]{1,0:T(8,128)(2,1)S(1)} %copy-done.1, bf16[1536,256]{1,0:T(8,128)(2,1)S(1)} %get-tuple-element.156.refs_2_, ...), custom_call_target="tpu_custom_call" | custom-call | flops 2752512 | bytes 1024 | tf_op jit(solution)/shard_map/attend_back/pallas_call | solution.py:54
  134.0 1.7 collective-permute-start.14
  136.6 5.4 %token_grad.1.refs_5_ = f32[2,512,768]{2,1,0:T(8,128)} custom-call(f32[512,768]{1,0:T(8,128)} %get-tuple-element.150.refs_0_, f32[512,768]{1,0:T(8,128)} %get-tuple-element.151.refs_1_, bf16[2,768,512]{2,1,0:T(8,128)(2,1)S(1)} %get-tuple-element.162.refs_2_.refs_8_, bf16[768,2304]{1,0:T(8,128)(2,1)} %refs_3_.1), custom_call_target="tpu_custom_call" | custom-call | flops 589824 | bytes 1024 | tf_op jit(solution)/shard_map/token_grad/pallas_call | solution.py:54
  142.0 1.8 collective-permute-done.11
  145.2 1.5 collective-permute-start.13
  147.6 8.0 %rest_grad.1 = (bf16[4,96,3200]{2,1,0:T(8,128)(2,1)}, bf16[4,96,3200]{2,1,0:T(8,128)(2,1)}) custom-call(s32[1]{0:T(128)} %bitcast.me_ref, bf16[4,2,96,512]{3,2,1,0:T(8,128)(2,1)S(1)} %get-tuple-element.167.refs_0_, bf16[4,2,96,512]{3,2,1,0:T(8,128)(2,1)S(1)} %get-tuple-element.168.refs_1_, bf16[512,768]{1,0:T(8,128)(2,1)} %get-tuple-element.154.refs_0_.refs_2_, ...), custom_call_target="tpu_custom_call" | custom-call | flops 3538944 | bytes 1024 | tf_op jit(solution)/shard_map/rest_grad/pallas_call | solution.py:54
  155.7 4.1 %collective-permute-done.13 = bf16[96,3072]{1,0:T(8,128)(2,1)S(1)} collective-permute-done((bf16[96,3072]{1,0:T(8,128)(2,1)S(1)}, bf16[96,3072]{1,0:T(8,128)(2,1)S(1)}, u32[]{:S(2)}, u32[]{:S(2)}) %collective-permute-start.13) | collective-permute-done | bytes 589856 | tf_op jit(solution)/shard_map/ppermute | solution.py:947
  159.7 1.6 collective-permute-done.12
  161.3 1.6 collective-permute-start.18
  163.6 2.7 %collective-permute-done.16 = bf16[4,96,3200]{2,1,0:T(8,128)(2,1)} collective-permute-done((bf16[4,96,3200]{2,1,0:T(8,128)(2,1)}, bf16[4,96,3200]{2,1,0:T(8,128)(2,1)}, u32[]{:S(2)}, u32[]{:S(2)}) %collective-permute-start.16) | collective-permute-done | bytes 2457632 | tf_op jit(solution)/shard_map/ppermute | solution.py:947
  166.3 2.0 fusion
  168.3 1.5 fusion.5
  170.7 1.1 collective-permute-start.17
  171.8 1.4 add_convert_fusion.3
  173.2 1.3 pad_maximum_fusion
  174.5 7.8 %collective-permute-done.18.refs_3_ = bf16[2,272,768]{2,1,0:T(8,128)(2,1)S(1)} collective-permute-done((bf16[2,272,768]{2,1,0:T(8,128)(2,1)S(1)}, bf16[2,272,768]{2,1,0:T(8,128)(2,1)S(1)}, u32[]{:S(2)}, u32[]{:S(2)}) %collective-permute-start.18) | collective-permute-done | bytes 835616 | tf_op jit(solution)/shard_map/ppermute | solution.py:956
  182.3 3.5 %collective-permute-done.17 = bf16[2,96,1536]{2,1,0:T(8,128)(2,1)S(1)} collective-permute-done((bf16[2,96,1536]{2,1,0:T(8,128)(2,1)S(1)}, bf16[2,96,1536]{2,1,0:T(8,128)(2,1)S(1)}, u32[]{:S(2)}, u32[]{:S(2)}) %collective-permute-start.17) | collective-permute-done | bytes 589856 | tf_op jit(solution)/shard_map/ppermute | solution.py:947
  186.6 1.7 collective-permute-start.25
  188.4 1.1 pad_maximum_fusion.1
  191.3 1.1 collective-permute-start.22
  192.4 4.7 %last.1 = (f32[2,512,768]{2,1,0:T(8,128)}, bf16[256,512]{1,0:T(8,128)(2,1)}) custom-call(bf16[2,272,768]{2,1,0:T(8,128)(2,1)S(1)} %copy-done.4, bf16[2,272,768]{2,1,0:T(8,128)(2,1)S(1)} %collective-permute-done.14.refs_1_, bf16[2,272,768]{2,1,0:T(8,128)(2,1)S(1)} %collective-permute-done.15.refs_2_, ...), custom_call_target="tpu_custom_call" | custom-call | flops 805306368 | bytes 8388608 | tf_op jit(solution)/shard_map/last/pallas_call | solution.py:54
  197.2 2.5 %collective-permute-start.26 = (bf16[24,3072]{1,0:T(8,128)(2,1)S(1)}, bf16[24,3072]{1,0:T(8,128)(2,1)S(1)}, u32[]{:S(2)}, u32[]{:S(2)}) collective-permute-start(bf16[24,3072]{1,0:T(8,128)(2,1)S(1)} %fusion.19), channel_id=1, source_target_pairs={{0,2},{1,3},{2,0},{3,1},{4,6},{5,7},{6,4},{7,5},{8,10},{9,11},{10,... | collective-permute-start | bytes 442376 | tf_op jit(solution)/shard_map/ppermute | solution.py:947
  201.7 3.8 %collective-permute-start.28 = (bf16[96,768]{1,0:T(8,128)(2,1)S(1)}, bf16[96,768]{1,0:T(8,128)(2,1)S(1)}, u32[]{:S(2)}, u32[]{:S(2)}) collective-permute-start(bf16[96,768]{1,0:T(8,128)(2,1)S(1)} %fusion.21), channel_id=1, source_target_pairs={{0,2},{1,3},{2,0},{3,1},{4,6},{5,7},{6,4},{7,5},{8,10},{9,11},{10,... | collective-permute-start | bytes 442376 | tf_op jit(solution)/shard_map/ppermute | solution.py:947
  206.5 4.7 %collective-permute-done.26 = bf16[24,3072]{1,0:T(8,128)(2,1)S(1)} collective-permute-done((bf16[24,3072]{1,0:T(8,128)(2,1)S(1)}, bf16[24,3072]{1,0:T(8,128)(2,1)S(1)}, u32[]{:S(2)}, u32[]{:S(2)}) %collective-permute-start.26) | collective-permute-done | bytes 147488 | tf_op jit(solution)/shard_map/ppermute | solution.py:947
  212.0 1.2 collective-permute-start.31
  213.3 4.0 %collective-permute-done.23 = bf16[2,24,3200]{2,1,0:T(8,128)(2,1)S(1)} collective-permute-done((bf16[2,24,3200]{2,1,0:T(8,128)(2,1)}, bf16[2,24,3200]{2,1,0:T(8,128)(2,1)S(1)}, u32[]{:S(2)}, u32[]{:S(2)}) %collective-permute-start.23) | collective-permute-done | bytes 307232 | tf_op jit(solution)/shard_map/ppermute | solution.py:947
  217.3 1.1 collective-permute-start.24
  219.2 5.9 %collective-permute-done.24.recv_ref = bf16[24,3200]{1,0:T(8,128)(2,1)S(1)} collective-permute-done((bf16[24,3200]{1,0:T(8,128)(2,1)S(1)}, bf16[24,3200]{1,0:T(8,128)(2,1)S(1)}, u32[]{:S(2)}, u32[]{:S(2)}) %collective-permute-start.24) | collective-permute-done | bytes 153632 | tf_op jit(solution)/shard_map/ppermute | solution.py:947
  (117 shorter events, 19.2 us)
Async XLA Ops:
  0.6 7.2 %copy-start.21 = (f32[768]{0:T(1024)S(1)}, f32[768]{0:T(1024)}, u32[]{:S(2)}) copy-start(f32[768]{0:T(1024)} %param.23) | copy-start | bytes 9220
  0.7 7.2 %copy-start.22 = (f32[768]{0:T(1024)S(1)}, f32[768]{0:T(1024)}, u32[]{:S(2)}) copy-start(f32[768]{0:T(1024)} %param.24) | copy-start | bytes 9220
  0.7 7.2 %copy-start.23 = (f32[768]{0:T(1024)S(1)}, f32[768]{0:T(1024)}, u32[]{:S(2)}) copy-start(f32[768]{0:T(1024)} %param.25) | copy-start | bytes 9220
  0.7 7.2 %copy-start.24 = (f32[768]{0:T(1024)S(1)}, f32[768]{0:T(1024)}, u32[]{:S(2)}) copy-start(f32[768]{0:T(1024)} %param.29) | copy-start | bytes 9220
  0.7 7.2 %copy-start.25 = (f32[768]{0:T(1024)S(1)}, f32[768]{0:T(1024)}, u32[]{:S(2)}) copy-start(f32[768]{0:T(1024)} %param.30) | copy-start | bytes 9220
  0.7 7.2 %copy-start.26 = (f32[768]{0:T(1024)S(1)}, f32[768]{0:T(1024)}, u32[]{:S(2)}) copy-start(f32[768]{0:T(1024)} %param.31) | copy-start | bytes 9220
  0.7 10.5 %copy-start.20 = (f32[2304]{0:T(1024)S(1)}, f32[2304]{0:T(1024)}, u32[]{:S(2)}) copy-start(f32[2304]{0:T(1024)} %param.21) | copy-start | bytes 27652
  3.4 13.0 %collective-permute-start = (bf16[272,768]{1,0:T(8,128)(2,1)}, bf16[272,768]{1,0:T(8,128)(2,1)}, u32[]{:S(2)}, u32[]{:S(2)}) collective-permute-start(bf16[272,768]{1,0:T(8,128)(2,1)} %get-tuple-element.109.refs_0_), channel_id=1, source_target_pairs={{0,1},{1,0},{2,3},{3,2},{4,5},{5,4},{6,7},{7,6},{8,9},{9,8},{10,11... | collective-permute-start | bytes 1253384 | tf_op jit(solution)/shard_map/ppermute | solution.py:953
  6.4 11.4 %collective-permute-start.1 = (bf16[272,768]{1,0:T(8,128)(2,1)}, bf16[272,768]{1,0:T(8,128)(2,1)}, u32[]{:S(2)}, u32[]{:S(2)}) collective-permute-start(bf16[272,768]{1,0:T(8,128)(2,1)} %get-tuple-element.109.refs_0_), channel_id=1, source_target_pairs={{1,2},{2,1},{5,6},{6,5},{9,10},{10,9},{13,14},{14,13},{17,18},{18,... | collective-permute-start | bytes 1253384 | tf_op jit(solution)/shard_map/ppermute | solution.py:953
  16.4 14.0 %collective-permute-start.3 = (bf16[272,768]{1,0:T(8,128)(2,1)}, bf16[272,768]{1,0:T(8,128)(2,1)}, u32[]{:S(2)}, u32[]{:S(2)}) collective-permute-start(bf16[272,768]{1,0:T(8,128)(2,1)} %collective-permute-done.refs_1_), channel_id=1, source_target_pairs={{1,2},{2,1},{5,6},{6,5},{9,10},{10,9},{13,14},{14,13},{17,18},{18,... | collective-permute-start | bytes 1253384 | tf_op jit(solution)/shard_map/ppermute | solution.py:956
  17.8 13.2 %collective-permute-start.2 = (bf16[272,768]{1,0:T(8,128)(2,1)}, bf16[272,768]{1,0:T(8,128)(2,1)}, u32[]{:S(2)}, u32[]{:S(2)}) collective-permute-start(bf16[272,768]{1,0:T(8,128)(2,1)} %collective-permute-done.1.refs_2_), channel_id=1, source_target_pairs={{0,1},{1,0},{2,3},{3,2},{4,5},{5,4},{6,7},{7,6},{8,9},{9,8},{10,11... | collective-permute-start | bytes 1253384 | tf_op jit(solution)/shard_map/ppermute | solution.py:956
  21.7 7.9 %copy-start.5 = (bf16[272,768]{1,0:T(8,128)(2,1)S(1)}, bf16[272,768]{1,0:T(8,128)(2,1)}, u32[]{:S(2)}) copy-start(bf16[272,768]{1,0:T(8,128)(2,1)} %get-tuple-element.135.refs_0_) | copy-start | bytes 1253380
  21.7 9.4 %copy-start.6 = (bf16[272,768]{1,0:T(8,128)(2,1)S(1)}, bf16[272,768]{1,0:T(8,128)(2,1)}, u32[]{:S(2)}) copy-start(bf16[272,768]{1,0:T(8,128)(2,1)} %get-tuple-element.109.refs_0_) | copy-start | bytes 1253380
  29.6 11.7 %collective-permute-start.4 = (bf16[272,768]{1,0:T(8,128)(2,1)S(1)}, bf16[272,768]{1,0:T(8,128)(2,1)S(1)}, u32[]{:S(2)}, u32[]{:S(2)}) collective-permute-start(bf16[272,768]{1,0:T(8,128)(2,1)S(1)} %copy-done.5), channel_id=1, source_target_pairs={{0,1},{1,0},{2,3},{3,2},{4,5},{5,4},{6,7},{7,6},{8,9},{9,8},{10,11... | collective-permute-start | bytes 1253384 | tf_op jit(solution)/shard_map/ppermute | solution.py:953
  29.7 11.6 %collective-permute-start.5 = (bf16[272,768]{1,0:T(8,128)(2,1)S(1)}, bf16[272,768]{1,0:T(8,128)(2,1)S(1)}, u32[]{:S(2)}, u32[]{:S(2)}) collective-permute-start(bf16[272,768]{1,0:T(8,128)(2,1)S(1)} %copy-done.5), channel_id=1, source_target_pairs={{1,2},{2,1},{5,6},{6,5},{9,10},{10,9},{13,14},{14,13},{17,18},{18,... | collective-permute-start | bytes 1253384 | tf_op jit(solution)/shard_map/ppermute | solution.py:953
  31.1 15.4 %copy-start.8 = (f32[3072,1]{1,0:T(8,128)S(1)}, f32[3072,1]{1,0:T(8,128)}, u32[]{:S(2)}) copy-start(f32[3072,1]{1,0:T(8,128)} %copy-done.7) | copy-start | bytes 36868
  41.3 26.1 %collective-permute-start.6 = (bf16[272,768]{1,0:T(8,128)(2,1)S(1)}, bf16[272,768]{1,0:T(8,128)(2,1)S(1)}, u32[]{:S(2)}, u32[]{:S(2)}) collective-permute-start(bf16[272,768]{1,0:T(8,128)(2,1)S(1)} %collective-permute-done.5.refs_2_), channel_id=1, source_target_pairs={{0,1},{1,0},{2,3},{3,2},{4,5},{5,4},{6,7},{7,6},{8,9},{9,8},{10,11... | collective-permute-start | bytes 1253384 | tf_op jit(solution)/shard_map/ppermute | solution.py:956
  45.6 21.8 %collective-permute-start.7 = (bf16[272,768]{1,0:T(8,128)(2,1)S(1)}, bf16[272,768]{1,0:T(8,128)(2,1)S(1)}, u32[]{:S(2)}, u32[]{:S(2)}) collective-permute-start(bf16[272,768]{1,0:T(8,128)(2,1)S(1)} %collective-permute-done.4.refs_1_), channel_id=1, source_target_pairs={{1,2},{2,1},{5,6},{6,5},{9,10},{10,9},{13,14},{14,13},{17,18},{18,... | collective-permute-start | bytes 1253384 | tf_op jit(solution)/shard_map/ppermute | solution.py:956
  102.2 4.7 %collective-permute-start.8 = (bf16[4,384,768]{2,1,0:T(8,128)(2,1)}, bf16[4,384,768]{2,1,0:T(8,128)(2,1)S(1)}, u32[]{:S(2)}, u32[]{:S(2)}) collective-permute-start(bf16[4,384,768]{2,1,0:T(8,128)(2,1)} %down_grad.2), channel_id=1, source_target_pairs={{0,4},{1,5},{2,6},{3,7},{4,0},{5,1},{6,2},{7,3},{8,12},{9,13},{10,... | collective-permute-start | bytes 7077896 | tf_op jit(solution)/shard_map/ppermute | solution.py:947
  106.3 4.9 %collective-permute-start.10 = (bf16[4,96,3072]{2,1,0:T(8,128)(2,1)}, bf16[4,96,3072]{2,1,0:T(8,128)(2,1)S(1)}, u32[]{:S(2)}, u32[]{:S(2)}) collective-permute-start(bf16[4,96,3072]{2,1,0:T(8,128)(2,1)} %get-tuple-element.146), channel_id=1, source_target_pairs={{0,4},{1,5},{2,6},{3,7},{4,0},{5,1},{6,2},{7,3},{8,12},{9,13},{10,... | collective-permute-start | bytes 7077896 | tf_op jit(solution)/shard_map/ppermute | solution.py:947
  111.1 7.3 %copy-start = (bf16[512,768]{1,0:T(8,128)(2,1)S(1)}, bf16[512,768]{1,0:T(8,128)(2,1)}, u32[]{:S(2)}) copy-start(bf16[512,768]{1,0:T(8,128)(2,1)} %get-tuple-element.154.refs_0_.refs_2_) | copy-start | bytes 2359300
  111.1 7.3 %copy-start.1 = (bf16[512,768]{1,0:T(8,128)(2,1)S(1)}, bf16[512,768]{1,0:T(8,128)(2,1)}, u32[]{:S(2)}) copy-start(bf16[512,768]{1,0:T(8,128)(2,1)} %get-tuple-element.155.refs_1_.refs_3_) | copy-start | bytes 2359300
  111.2 7.1 %copy-start.3 = (bf16[12,256,512]{2,1,0:T(8,128)(2,1)S(1)}, bf16[12,256,512]{2,1,0:T(8,128)(2,1)}, u32[]{:S(2)}) copy-start(bf16[12,256,512]{2,1,0:T(8,128)(2,1)} %get-tuple-element.159.refs_5_) | copy-start | bytes 9437188
  115.3 28.5 %collective-permute-start.11 = (bf16[2,96,3072]{2,1,0:T(8,128)(2,1)}, bf16[2,96,3072]{2,1,0:T(8,128)(2,1)S(1)}, u32[]{:S(2)}, u32[]{:S(2)}) collective-permute-start(bf16[2,96,3072]{2,1,0:T(8,128)(2,1)} %get-tuple-element.153), channel_id=1, source_target_pairs={{0,16},{1,17},{2,18},{3,19},{4,20},{5,21},{6,22},{7,23},{8,24},{9,... | collective-permute-start | bytes 3538952 | tf_op jit(solution)/shard_map/ppermute | solution.py:947
  116.8 28.0 %collective-permute-start.9 = (bf16[2,384,768]{2,1,0:T(8,128)(2,1)S(1)}, bf16[2,384,768]{2,1,0:T(8,128)(2,1)S(1)}, u32[]{:S(2)}, u32[]{:S(2)}) collective-permute-start(bf16[2,384,768]{2,1,0:T(8,128)(2,1)S(1)} %copy-done.27), channel_id=1, source_target_pairs={{0,8},{1,9},{2,10},{3,11},{4,12},{5,13},{6,14},{7,15},{8,0},{9,1},... | collective-permute-start | bytes 3538952 | tf_op jit(solution)/shard_map/ppermute | solution.py:947
  134.0 21.7 %collective-permute-start.14 = (bf16[2,272,768]{2,1,0:T(8,128)(2,1)}, bf16[2,272,768]{2,1,0:T(8,128)(2,1)S(1)}, u32[]{:S(2)}, u32[]{:S(2)}) collective-permute-start(bf16[2,272,768]{2,1,0:T(8,128)(2,1)} %get-tuple-element.186.refs_0_), channel_id=1, source_target_pairs={{0,1},{1,0},{2,3},{3,2},{4,5},{5,4},{6,7},{7,6},{8,9},{9,8},{10,11... | collective-permute-start | bytes 2506760 | tf_op jit(solution)/shard_map/ppermute | solution.py:953
  135.7 20.0 %collective-permute-start.15 = (bf16[2,272,768]{2,1,0:T(8,128)(2,1)}, bf16[2,272,768]{2,1,0:T(8,128)(2,1)S(1)}, u32[]{:S(2)}, u32[]{:S(2)}) collective-permute-start(bf16[2,272,768]{2,1,0:T(8,128)(2,1)} %get-tuple-element.186.refs_0_), channel_id=1, source_target_pairs={{1,2},{2,1},{5,6},{6,5},{9,10},{10,9},{13,14},{14,13},{17,18},{18,... | collective-permute-start | bytes 2506760 | tf_op jit(solution)/shard_map/ppermute | solution.py:953
  136.6 8.2 %copy-start.10 = (bf16[2,96,3072]{2,1,0:T(8,128)(2,1)S(1)}, bf16[2,96,3072]{2,1,0:T(8,128)(2,1)}, u32[]{:S(2)}) copy-start(bf16[2,96,3072]{2,1,0:T(8,128)(2,1)} %get-tuple-element.164) | copy-start | bytes 3538948
  145.2 14.5 %collective-permute-start.13 = (bf16[96,3072]{1,0:T(8,128)(2,1)S(1)}, bf16[96,3072]{1,0:T(8,128)(2,1)S(1)}, u32[]{:S(2)}, u32[]{:S(2)}) collective-permute-start(bf16[96,3072]{1,0:T(8,128)(2,1)S(1)} %get-tuple-element.206), channel_id=1, source_target_pairs={{0,8},{1,9},{2,10},{3,11},{4,12},{5,13},{6,14},{7,15},{8,0},{9,1},... | collective-permute-start | bytes 1769480 | tf_op jit(solution)/shard_map/ppermute | solution.py:947
  147.0 14.3 %collective-permute-start.12 = (bf16[384,768]{1,0:T(8,128)(2,1)S(1)}, bf16[384,768]{1,0:T(8,128)(2,1)S(1)}, u32[]{:S(2)}, u32[]{:S(2)}) collective-permute-start(bf16[384,768]{1,0:T(8,128)(2,1)S(1)} %get-tuple-element.208), channel_id=1, source_target_pairs={{0,16},{1,17},{2,18},{3,19},{4,20},{5,21},{6,22},{7,23},{8,24},{9,... | collective-permute-start | bytes 1769480 | tf_op jit(solution)/shard_map/ppermute | solution.py:947
  161.3 5.0 %collective-permute-start.16 = (bf16[4,96,3200]{2,1,0:T(8,128)(2,1)}, bf16[4,96,3200]{2,1,0:T(8,128)(2,1)}, u32[]{:S(2)}, u32[]{:S(2)}) collective-permute-start(bf16[4,96,3200]{2,1,0:T(8,128)(2,1)} %get-tuple-element.179), channel_id=1, source_target_pairs={{0,4},{1,5},{2,6},{3,7},{4,0},{5,1},{6,2},{7,3},{8,12},{9,13},{10,... | collective-permute-start | bytes 7372808 | tf_op jit(solution)/shard_map/ppermute | solution.py:947
  161.3 21.0 %collective-permute-start.18 = (bf16[2,272,768]{2,1,0:T(8,128)(2,1)S(1)}, bf16[2,272,768]{2,1,0:T(8,128)(2,1)S(1)}, u32[]{:S(2)}, u32[]{:S(2)}) collective-permute-start(bf16[2,272,768]{2,1,0:T(8,128)(2,1)S(1)} %collective-permute-done.15.refs_2_), channel_id=1, source_target_pairs={{0,1},{1,0},{2,3},{3,2},{4,5},{5,4},{6,7},{7,6},{8,9},{9,8},{10,11... | collective-permute-start | bytes 2506760 | tf_op jit(solution)/shard_map/ppermute | solution.py:956
  162.9 19.4 %collective-permute-start.19 = (bf16[2,272,768]{2,1,0:T(8,128)(2,1)S(1)}, bf16[2,272,768]{2,1,0:T(8,128)(2,1)S(1)}, u32[]{:S(2)}, u32[]{:S(2)}) collective-permute-start(bf16[2,272,768]{2,1,0:T(8,128)(2,1)S(1)} %collective-permute-done.14.refs_1_), channel_id=1, source_target_pairs={{1,2},{2,1},{5,6},{6,5},{9,10},{10,9},{13,14},{14,13},{17,18},{18,... | collective-permute-start | bytes 2506760 | tf_op jit(solution)/shard_map/ppermute | solution.py:956
  169.8 16.5 %collective-permute-start.20 = (bf16[2,96,1664]{2,1,0:T(8,128)(2,1)S(1)}, bf16[2,96,1664]{2,1,0:T(8,128)(2,1)S(1)}, u32[]{:S(2)}, u32[]{:S(2)}) collective-permute-start(bf16[2,96,1664]{2,1,0:T(8,128)(2,1)S(1)} %get-tuple-element.203), channel_id=1, source_target_pairs={{0,16},{1,17},{2,18},{3,19},{4,20},{5,21},{6,22},{7,23},{8,24},{9,... | collective-permute-start | bytes 1916936 | tf_op jit(solution)/shard_map/ppermute | solution.py:947
  170.7 15.1 %collective-permute-start.17 = (bf16[2,96,1536]{2,1,0:T(8,128)(2,1)S(1)}, bf16[2,96,1536]{2,1,0:T(8,128)(2,1)S(1)}, u32[]{:S(2)}, u32[]{:S(2)}) collective-permute-start(bf16[2,96,1536]{2,1,0:T(8,128)(2,1)S(1)} %fusion.5), channel_id=1, source_target_pairs={{0,8},{1,9},{2,10},{3,11},{4,12},{5,13},{6,14},{7,15},{8,0},{9,1},... | collective-permute-start | bytes 1769480 | tf_op jit(solution)/shard_map/ppermute | solution.py:947
  174.5 12.0 %copy-start.16 = (bf16[96,3072]{1,0:T(8,128)(2,1)S(1)}, bf16[96,3072]{1,0:T(8,128)(2,1)}, u32[]{:S(2)}) copy-start(bf16[96,3072]{1,0:T(8,128)(2,1)} %copy-done.15) | copy-start | bytes 1769476
  186.6 10.4 %collective-permute-start.25 = (bf16[2,24,3072]{2,1,0:T(8,128)(2,1)S(1)}, bf16[2,24,3072]{2,1,0:T(8,128)(2,1)S(1)}, u32[]{:S(2)}, u32[]{:S(2)}) collective-permute-start(bf16[2,24,3072]{2,1,0:T(8,128)(2,1)S(1)} %get-tuple-element.214), channel_id=1, source_target_pairs={{0,1},{1,0},{2,3},{3,2},{4,5},{5,4},{6,7},{7,6},{8,9},{9,8},{10,11... | collective-permute-start | bytes 884744 | tf_op jit(solution)/shard_map/ppermute | solution.py:947
  189.4 16.1 %collective-permute-start.21 = (bf16[96,1536]{1,0:T(8,128)(2,1)S(1)}, bf16[96,1536]{1,0:T(8,128)(2,1)S(1)}, u32[]{:S(2)}, u32[]{:S(2)}) collective-permute-start(bf16[96,1536]{1,0:T(8,128)(2,1)S(1)} %get-tuple-element.216), channel_id=1, source_target_pairs={{0,16},{1,17},{2,18},{3,19},{4,20},{5,21},{6,22},{7,23},{8,24},{9,... | collective-permute-start | bytes 884744 | tf_op jit(solution)/shard_map/ppermute | solution.py:947
  190.5 11.2 %collective-permute-start.27 = (bf16[2,96,768]{2,1,0:T(8,128)(2,1)S(1)}, bf16[2,96,768]{2,1,0:T(8,128)(2,1)S(1)}, u32[]{:S(2)}, u32[]{:S(2)}) collective-permute-start(bf16[2,96,768]{2,1,0:T(8,128)(2,1)S(1)} %get-tuple-element.212), channel_id=1, source_target_pairs={{0,1},{1,0},{2,3},{3,2},{4,5},{5,4},{6,7},{7,6},{8,9},{9,8},{10,11... | collective-permute-start | bytes 884744 | tf_op jit(solution)/shard_map/ppermute | solution.py:947
  191.3 14.3 %collective-permute-start.22 = (bf16[96,1664]{1,0:T(8,128)(2,1)S(1)}, bf16[96,1664]{1,0:T(8,128)(2,1)S(1)}, u32[]{:S(2)}, u32[]{:S(2)}) collective-permute-start(bf16[96,1664]{1,0:T(8,128)(2,1)S(1)} %get-tuple-element.210), channel_id=1, source_target_pairs={{0,8},{1,9},{2,10},{3,11},{4,12},{5,13},{6,14},{7,15},{8,0},{9,1},... | collective-permute-start | bytes 958472 | tf_op jit(solution)/shard_map/ppermute | solution.py:947
  197.1 2.5 %collective-permute-start.29 = (bf16[256,512]{1,0:T(8,128)(2,1)}, bf16[256,512]{1,0:T(8,128)(2,1)S(1)}, u32[]{:S(2)}, u32[]{:S(2)}) collective-permute-start(bf16[256,512]{1,0:T(8,128)(2,1)} %get-tuple-element.202), channel_id=1, source_target_pairs={{0,4},{1,5},{2,6},{3,7},{4,0},{5,1},{6,2},{7,3},{8,12},{9,13},{10,... | collective-permute-start | bytes 786440 | tf_op jit(solution)/shard_map/ppermute | solution.py:947
  197.2 14.0 %collective-permute-start.26 = (bf16[24,3072]{1,0:T(8,128)(2,1)S(1)}, bf16[24,3072]{1,0:T(8,128)(2,1)S(1)}, u32[]{:S(2)}, u32[]{:S(2)}) collective-permute-start(bf16[24,3072]{1,0:T(8,128)(2,1)S(1)} %fusion.19), channel_id=1, source_target_pairs={{0,2},{1,3},{2,0},{3,1},{4,6},{5,7},{6,4},{7,5},{8,10},{9,11},{10,... | collective-permute-start | bytes 442376 | tf_op jit(solution)/shard_map/ppermute | solution.py:947
  200.6 11.3 %collective-permute-start.30 = (bf16[256,512]{1,0:T(8,128)(2,1)S(1)}, bf16[256,512]{1,0:T(8,128)(2,1)S(1)}, u32[]{:S(2)}, u32[]{:S(2)}) collective-permute-start(bf16[256,512]{1,0:T(8,128)(2,1)S(1)} %add_convert_fusion.13), channel_id=1, source_target_pairs={{0,8},{1,9},{2,10},{3,11},{4,12},{5,13},{6,14},{7,15},{8,0},{9,1},... | collective-permute-start | bytes 786440 | tf_op jit(solution)/shard_map/ppermute | solution.py:947
  201.7 16.7 %collective-permute-start.28 = (bf16[96,768]{1,0:T(8,128)(2,1)S(1)}, bf16[96,768]{1,0:T(8,128)(2,1)S(1)}, u32[]{:S(2)}, u32[]{:S(2)}) collective-permute-start(bf16[96,768]{1,0:T(8,128)(2,1)S(1)} %fusion.21), channel_id=1, source_target_pairs={{0,2},{1,3},{2,0},{3,1},{4,6},{5,7},{6,4},{7,5},{8,10},{9,11},{10,... | collective-permute-start | bytes 442376 | tf_op jit(solution)/shard_map/ppermute | solution.py:947
  206.5 10.8 %copy-start.17 = (bf16[2,24,3200]{2,1,0:T(8,128)(2,1)S(1)}, bf16[2,24,3200]{2,1,0:T(8,128)(2,1)}, u32[]{:S(2)}) copy-start(bf16[2,24,3200]{2,1,0:T(8,128)(2,1)} %get-tuple-element.190) | copy-start | bytes 921604
  206.5 10.8 %collective-permute-start.23 = (bf16[2,24,3200]{2,1,0:T(8,128)(2,1)}, bf16[2,24,3200]{2,1,0:T(8,128)(2,1)S(1)}, u32[]{:S(2)}, u32[]{:S(2)}) collective-permute-start(bf16[2,24,3200]{2,1,0:T(8,128)(2,1)} %get-tuple-element.191), channel_id=1, source_target_pairs={{0,1},{1,0},{2,3},{3,2},{4,5},{5,4},{6,7},{7,6},{8,9},{9,8},{10,11... | collective-permute-start | bytes 921608 | tf_op jit(solution)/shard_map/ppermute | solution.py:947
  212.0 13.9 %collective-permute-start.31 = (bf16[256,512]{1,0:T(8,128)(2,1)S(1)}, bf16[256,512]{1,0:T(8,128)(2,1)S(1)}, u32[]{:S(2)}, u32[]{:S(2)}) collective-permute-start(bf16[256,512]{1,0:T(8,128)(2,1)S(1)} %add_convert_fusion.12), channel_id=1, source_target_pairs={{0,16},{1,17},{2,18},{3,19},{4,20},{5,21},{6,22},{7,23},{8,24},{9,... | collective-permute-start | bytes 786440 | tf_op jit(solution)/shard_map/ppermute | solution.py:947
  217.3 7.7 %collective-permute-start.24 = (bf16[24,3200]{1,0:T(8,128)(2,1)S(1)}, bf16[24,3200]{1,0:T(8,128)(2,1)S(1)}, u32[]{:S(2)}, u32[]{:S(2)}) collective-permute-start(bf16[24,3200]{1,0:T(8,128)(2,1)S(1)} %get-tuple-element.217), channel_id=1, source_target_pairs={{0,2},{1,3},{2,0},{3,1},{4,6},{5,7},{6,4},{7,5},{8,10},{9,11},{10,... | collective-permute-start | bytes 460808 | tf_op jit(solution)/shard_map/ppermute | solution.py:947
  (12 other events, 39.6 us)
